TPU v7x, 768 devices: a whole 4x8x12 slice. The times are simulated.
768 devices in a mesh: lat: 48 (over x_hi, z, core), lon: 16 (over x_lo, y).
Axes of the slice: x: 4 (x_hi: 2, x_lo: 2; x = x_hi * 2 + x_lo), y: 8, z: 12, core: 2. Of those that a mesh axis runs over, the one named last changes fastest.
Arguments:
- tokens: bfloat16 [4, 288, 384, 192], P(None, 'lat', 'lon'), may hold values from -6 to 6
- cotangent: bfloat16 [4, 288, 384, 192], P(None, 'lat', 'lon'), may hold values from -6 to 6
- norm_gain: float32 [192], replicated, may hold values from 0.1 to 1.9
- inproj_weight: bfloat16 [192, 576], replicated, may hold values from -0.4375 to 0.4375
- outproj_weight: bfloat16 [192, 192], replicated, may hold values from -0.4375 to 0.4375
- bias: float32 [2, 48, 6, 144, 144], P(None, 'lat'), may hold values from -4 to 4
Outputs:
- grad_input: bfloat16 [4, 288, 384, 192], P(None, 'lat', 'lon')
- bias_grad: float32 [2, 48, 6, 144, 144], P(None, 'lat', None, 'lon')
All inputs are finite; a program needn't handle non-finite values.
Results may differ from a plain program's by a relative error of at most 0.017.
Values may be sent and summed in bfloat16 or wider, within the bound.
A program may use at most 32 MiB of HBM per device.

v0:
```python
import jax
import jax.numpy as jnp
from jax import lax
from jax.sharding import PartitionSpec as P

WZ = 2
WH = 6
WW = 12
ZWIN = 2


epsilon = 1e-05


def from_behind(value, axis, by):
    devices = lax.axis_size(axis)
    return lax.ppermute(value, axis, [(i, (i + by) % devices) for i in range(devices)])


def cut_along(value, dim, devices):
    before, after = (value.shape[:dim], value.shape[dim + 1 :])
    return jnp.moveaxis(value.reshape(*before, devices, -1, *after), dim, 0)


def sum_at_owner(value, axis, dim):
    blocks = cut_along(value, dim, lax.axis_size(axis))
    arrived = lax.all_to_all(blocks, axis, split_axis=0, concat_axis=0, tiled=True)
    return arrived.astype(jnp.float32).sum(axis=0)


def allowed_pairs(level_win, lat_window, level_total, row_total):
    positions = jnp.arange(WZ * WH * WW, dtype=jnp.int32)
    level_pos = level_win * WZ + positions // (WH * WW)
    row_pos = lat_window * WH + positions // WW % WH
    labels = (level_pos >= level_total - WZ // 2).astype(jnp.int32) * 2 + (
        row_pos >= row_total - WH // 2
    ).astype(jnp.int32)
    return labels[:, None] == labels[None, :]


def to_windows(field):
    level_total, row_total, col_total, channels = field.shape
    blocks = field.reshape(
        level_total // WZ, WZ, row_total // WH, WH, col_total // WW, WW, channels
    )
    blocks = blocks.transpose(0, 2, 4, 1, 3, 5, 6)
    return blocks.reshape(
        level_total // WZ, row_total // WH, col_total // WW, WZ * WH * WW, channels
    )


def from_windows(blocks):
    level_win, lat_win, lon_win, token_count, channels = blocks.shape
    field = blocks.reshape(level_win, lat_win, lon_win, WZ, WH, WW, channels)
    field = field.transpose(0, 3, 1, 4, 2, 5, 6)
    return field.reshape(level_win * WZ, lat_win * WH, lon_win * WW, channels)


def band_backward(band_in, band_grad, gain, inproj_weight, outproj_weight, band_bias, allowed):
    window_count, token_count, channels = band_in.shape
    head_count = band_bias.shape[0]
    head_dim = channels // head_count
    scaling = head_dim ** (-0.5)
    floats = band_in.astype(jnp.float32)
    centred = floats - jnp.mean(floats, axis=-1, keepdims=True)
    inverse_rms = lax.rsqrt(jnp.mean(centred * centred, axis=-1, keepdims=True) + epsilon)
    standard = centred * inverse_rms
    normed = (standard * gain).astype(jnp.bfloat16)
    projected = jnp.dot(
        normed.reshape(-1, channels), inproj_weight, preferred_element_type=jnp.float32
    ).astype(jnp.bfloat16)
    projected = projected.reshape(window_count, token_count, 3, head_count, head_dim)
    query_rows = projected[:, :, 0]
    key_rows = projected[:, :, 1]
    value_rows = projected[:, :, 2]
    scores = (
        jnp.einsum("nihd,njhd->nhij", query_rows, key_rows, preferred_element_type=jnp.float32)
        * scaling
        + band_bias[None]
    )
    weights = jnp.where(allowed[None, None], jnp.exp(scores), 0.0)
    probabilities = weights / jnp.sum(weights, axis=-1, keepdims=True)
    upstream = lax.dot_general(
        band_grad.reshape(-1, channels),
        outproj_weight,
        (((1,), (1,)), ((), ())),
        preferred_element_type=jnp.float32,
    ).astype(jnp.bfloat16)
    upstream = upstream.reshape(window_count, token_count, head_count, head_dim)
    dprobs = jnp.einsum("nihd,njhd->nhij", upstream, value_rows, preferred_element_type=jnp.float32)
    inner_sum = jnp.sum(probabilities * dprobs, axis=-1, keepdims=True)
    dscores = probabilities * (dprobs - inner_sum)
    bias_part = jnp.sum(dscores, axis=0)
    probs_low = probabilities.astype(jnp.bfloat16)
    dscores_low = dscores.astype(jnp.bfloat16)
    dquery = (
        jnp.einsum("nhij,njhd->nihd", dscores_low, key_rows, preferred_element_type=jnp.float32)
        * scaling
    ).astype(jnp.bfloat16)
    dkeys = (
        jnp.einsum("nhij,nihd->njhd", dscores_low, query_rows, preferred_element_type=jnp.float32)
        * scaling
    ).astype(jnp.bfloat16)
    dvalues = jnp.einsum(
        "nhij,nihd->njhd", probs_low, upstream, preferred_element_type=jnp.float32
    ).astype(jnp.bfloat16)
    dprojected = jnp.stack([dquery, dkeys, dvalues], axis=2).reshape(-1, 3 * channels)
    dnormed = lax.dot_general(
        dprojected, inproj_weight, (((1,), (1,)), ((), ())), preferred_element_type=jnp.float32
    )
    dnormed = dnormed.reshape(window_count, token_count, channels)
    scaled = dnormed * gain
    grad_moved = inverse_rms * (
        scaled
        - jnp.mean(scaled, axis=-1, keepdims=True)
        - standard * jnp.mean(scaled * standard, axis=-1, keepdims=True)
    )
    return (grad_moved.astype(jnp.bfloat16), bias_part)


def rows_in(stacked):
    rim_rows = stacked[:, :, : WH // 2]
    received = from_behind(rim_rows, "lat", -1)
    return jnp.concatenate([stacked[:, :, WH // 2 :], received], axis=2)


def cols_in(stacked):
    rim_cols = stacked[:, :, :, : WW // 2]
    received = from_behind(rim_cols, "lon", -1)
    return jnp.concatenate([stacked[:, :, :, WW // 2 :], received], axis=3)


def rows_out(field_part):
    rim_rows = field_part[:, field_part.shape[1] - WH // 2 :]
    received = from_behind(rim_rows, "lat", 1)
    return jnp.concatenate([received, field_part[:, : field_part.shape[1] - WH // 2]], axis=1)


def cols_out(field_part):
    rim_cols = field_part[:, :, field_part.shape[2] - WW // 2 :]
    received = from_behind(rim_cols, "lon", 1)
    return jnp.concatenate([received, field_part[:, :, : field_part.shape[2] - WW // 2]], axis=2)


def local(tokens, cotangent, norm_gain, inproj_weight, outproj_weight, bias):
    level_total = tokens.shape[0]
    row_total = tokens.shape[1] * lax.axis_size("lat")
    lat_local = tokens.shape[1] // WH
    stacked = jnp.stack([tokens, cotangent])
    moved = cols_in(rows_in(stacked))
    moved = jnp.roll(moved, -(WZ // 2), axis=1)
    in_windows = to_windows(moved[0])
    grad_windows = to_windows(moved[1])
    lat_windows = lax.axis_index("lat") * lat_local + jnp.arange(lat_local, dtype=jnp.int32)
    grad_levels = []
    bias_levels = []
    for level_win in range(ZWIN):

        def one_band(operands, level_win=level_win):
            band_in, band_grad, band_bias, lat_window = operands
            allowed = allowed_pairs(level_win, lat_window, level_total, row_total)
            return band_backward(
                band_in, band_grad, norm_gain, inproj_weight, outproj_weight, band_bias, allowed
            )

        grad_blocks, bias_parts = lax.map(
            one_band, (in_windows[level_win], grad_windows[level_win], bias[level_win], lat_windows)
        )
        grad_levels.append(grad_blocks)
        bias_levels.append(bias_parts)
    bias_local = jnp.stack(bias_levels)
    bias_local = sum_at_owner(bias_local.astype(jnp.bfloat16), "lon", 3)
    grad_field = from_windows(jnp.stack(grad_levels))
    grad_field = jnp.roll(grad_field, WZ // 2, axis=0)
    grad_input = cols_out(rows_out(grad_field))
    return (grad_input, bias_local)


def solution(mesh):
    placed = (
        P(None, "lat", "lon", None),
        P(None, "lat", "lon", None),
        P(),
        P(),
        P(),
        P(None, "lat", None, None, None),
    )
    return jax.shard_map(
        local,
        mesh=mesh,
        in_specs=placed,
        out_specs=(P(None, "lat", "lon", None), P(None, "lat", None, "lon", None)),
        check_vma=False,
    )
```

profile of v0, /device:TPU:2, one launch (start us, length us, event | category | flops | bytes accessed | tf_op | source)
XLA Modules:
  0.0 100.3 jit_solution(5579000355730609144)
XLA Ops:
  0.6 1.3 %fusion.22 = (bf16[2,4,3,24,192]{4,3,2,1,0:T(8,128)(2,1)S(1)}, bf16[2,4,3,24,192]{4,3,2,1,0:T(8,128)(2,1)S(1)}) fusion(bf16[1,4,6,24,192]{4,3,2,1,0:T(8,128)(2,1)} %bitcast.132, bf16[1,4,6,24,192]{4,3,2,1,0:T(8,128)(2,1)} %bitcast.133), kind=kLoop, calls=%fused_computation.52 | loop fusion | flops 221184 | bytes 884736 | tf_op jit(solution)/shard_map/stack | solution.py:149
  1.9 15.6 %collective-permute-start = (bf16[2,4,3,24,192]{4,3,2,1,0:T(8,128)(2,1)S(1)}, bf16[2,4,3,24,192]{4,3,2,1,0:T(8,128)(2,1)S(1)}, u32[]{:S(2)}, u32[]{:S(2)}) collective-permute-start(bf16[2,4,3,24,192]{4,3,2,1,0:T(8,128)(2,1)S(1)} %get-tuple-element.89), channel_id=1, source_target_pairs={{0,752},{16,0},{32,16},{48,32},{64,48},{80,64},{96,80},{112,96},{1... | collective-permute-start | bytes 663560 | tf_op jit(solution)/shard_map/ppermute | solution.py:17
  17.5 1.6 %slice_bitcast_fusion.1 = (f32[6,144,144]{2,1,0:T(8,128)S(1)}, f32[6,144,144]{2,1,0:T(8,128)S(1)}) fusion(f32[2,1,6,144,144]{4,3,2,1,0:T(8,128)} %param.11), kind=kLoop, calls=%fused_computation.37 | loop fusion | bytes 1990656 | tf_op jit(solution)/shard_map/while/body/eval_jaxpr/add | solution.py:77
  19.1 1.4 %copy.162 = f32[6,144,144]{1,2,0:T(8,128)} copy(f32[6,144,144]{2,1,0:T(8,128)S(1)} %get-tuple-element.69) | data formatting | bytes 995328 | tf_op jit(solution)/shard_map/while/body/eval_jaxpr/add | solution.py:77
  20.5 0.7 broadcast_compare_fusion
  21.2 1.4 %copy.136 = f32[6,144,144]{1,2,0:T(8,128)} copy(f32[6,144,144]{2,1,0:T(8,128)S(1)} %get-tuple-element.68) | data formatting | bytes 995328 | tf_op jit(solution)/shard_map/while/body/eval_jaxpr/add | solution.py:77
  22.6 0.7 broadcast_compare_fusion.1
  23.3 6.2 %collective-permute-start.1 = (bf16[2,4,6,6,192]{4,3,2,1,0:T(8,128)(2,1)S(1)}, bf16[2,4,6,6,192]{4,3,2,1,0:T(8,128)(2,1)S(1)}, u32[]{:S(2)}, u32[]{:S(2)}) collective-permute-start(bf16[2,4,6,6,192]{4,3,2,1,0:T(8,128)(2,1)S(1)} %pad_maximum_fusion.6), channel_id=1, source_target_pairs={{0,15},{1,0},{2,1},{3,2},{4,3},{5,4},{6,5},{7,6},{8,7},{9,8},{10,9... | collective-permute-start | bytes 331784 | tf_op jit(solution)/shard_map/ppermute | solution.py:17
  29.8 3.0 %collective-permute-done.1 = bf16[2,4,6,6,192]{4,3,2,1,0:T(8,128)(2,1)S(1)} collective-permute-done((bf16[2,4,6,6,192]{4,3,2,1,0:T(8,128)(2,1)S(1)}, bf16[2,4,6,6,192]{4,3,2,1,0:T(8,128)(2,1)S(1)}, u32[]{:S(2)}, u32[]{:S(2)}) %collective-permute-start.1) | collective-permute-done | bytes 110624 | tf_op jit(solution)/shard_map/ppermute | solution.py:17
  33.2 0.2 reshape_squeeze.6
  33.5 0.2 fusion.41
  33.7 0.6 multiply_reduce_fusion.5
  34.4 0.5 multiply_reduce_fusion.3
  34.9 0.2 copy.157
  35.1 0.2 slice_convert_fusion.1
  35.5 0.2 copy.155
  36.1 0.3 convolution_convert_fusion
  36.5 0.2 copy.159
  36.7 0.2 reshape.370
  37.0 1.2 %fusion.51 = (bf16[2,144,1,6,32]{1,0,4,3,2:T(2,128)(2,1)}, bf16[2,144,1,6,32]{1,0,4,3,2:T(2,128)(2,1)}, bf16[2,144,1,6,32]{1,0,4,3,2:T(2,128)(2,1)}) fusion(bf16[2,144,3,6,32]{1,0,4,3,2:T(2,128)(2,1)S(1)} %reshape.370), kind=kLoop, calls=%fused_computation.129 | loop fusion | bytes 663552 | tf_op jit(solution)/shard_map/while/body/eval_jaxpr/slice | solution.py:75
  38.3 0.2 reshape_squeeze.7
  38.6 0.9 fusion.53
  39.5 0.2 convolution_convert_fusion.4
  40.0 1.4 %fusion.28 = f32[2,6,144,144]{2,3,1,0:T(8,128)S(1)} fusion(bf16[2,144,1,6,32]{1,0,4,3,2:T(2,128)(2,1)} %get-tuple-element.83, bf16[2,144,6,32]{1,0,3,2:T(2,128)(2,1)S(1)} %reshape.372), kind=kOutput, calls=%fused_computation.76 | convolution fusion | flops 15925248 | bytes 1216512 | tf_op jit(solution)/shard_map/while/body/eval_jaxpr/nihd,njhd->nhij/dot_general | solution.py:90
  41.4 3.9 %multiply_reduce_fusion = (f32[2,6,144]{2,1,0:T(8,128)}, f32[2,6,144,144]{2,3,1,0:T(8,128)}) fusion(f32[2,6,144,144]{2,3,1,0:T(8,128)S(1)} %fusion.28, f32[6,144,144]{1,2,0:T(8,128)} %copy.162, pred[144,144]{0,1:T(8,128)(4,1)} %broadcast_compare_fusion, bf16[2,144,1,6,32]{1,0,4,3,2:T(2,128)(2,1)S(1)} %copy-done.10, bf16[2,144,1,6,32]{1,0,4,3,2:T(2,128)(2,1)S(1)} %copy-done.8), kind=kOutput, calls=%fused_computation.2 | convolution fusion | flops 17418384 | bytes 2737152 | tf_op jit(solution)/shard_map/while/body/eval_jaxpr/div | solution.py:82
  45.3 2.7 %fusion.5 = bf16[2,144,1,6,32]{1,4,3,0,2:T(8,128)(2,1)} fusion(f32[2,6,144,144]{2,3,1,0:T(8,128)} %get-tuple-element.95, bf16[2,144,6,32]{1,0,3,2:T(2,128)(2,1)S(1)} %reshape.372), kind=kOutput, calls=%fused_computation.25 | convolution fusion | flops 16229376 | bytes 1216512 | tf_op jit(solution)/shard_map/while/body/eval_jaxpr/nhij,nihd->njhd/dot_general | solution.py:104
  48.0 0.5 fusion.18
  48.5 0.4 copy-done.11
  48.9 1.1 %fusion.6 = bf16[2,144,1,6,32]{1,4,3,0,2:T(8,128)(2,1)} fusion(bf16[2,6,144,144]{2,3,1,0:T(8,128)(2,1)S(1)} %get-tuple-element.67, bf16[2,144,1,6,32]{1,0,4,3,2:T(2,128)(2,1)S(1)} %copy-done.11), kind=kOutput, calls=%fused_computation.26 | convolution fusion | flops 16035840 | bytes 718848 | tf_op jit(solution)/shard_map/while/body/eval_jaxpr/nhij,nihd->njhd/dot_general | solution.py:101
  50.0 0.9 fusion.7
  51.3 0.2 copy.129
  51.9 0.3 convolution_convert_fusion.1
  52.3 0.2 copy.133
  52.5 0.2 reshape.367
  52.8 1.3 %fusion.50 = (bf16[2,144,1,6,32]{1,0,4,3,2:T(2,128)(2,1)}, bf16[2,144,1,6,32]{1,0,4,3,2:T(2,128)(2,1)S(1)}, bf16[2,144,1,6,32]{1,0,4,3,2:T(2,128)(2,1)}) fusion(bf16[2,144,3,6,32]{1,0,4,3,2:T(2,128)(2,1)S(1)} %reshape.367), kind=kLoop, calls=%fused_computation.128 | loop fusion | bytes 663552 | tf_op jit(solution)/shard_map/while/body/eval_jaxpr/slice | solution.py:75
  54.1 0.2 convolution_convert_fusion.5
  54.6 1.4 %fusion.29 = f32[2,6,144,144]{2,3,1,0:T(8,128)S(1)} fusion(bf16[2,144,1,6,32]{1,0,4,3,2:T(2,128)(2,1)} %get-tuple-element.80, bf16[2,144,6,32]{1,0,3,2:T(2,128)(2,1)S(1)} %reshape.369), kind=kOutput, calls=%fused_computation.80 | convolution fusion | flops 15925248 | bytes 1216512 | tf_op jit(solution)/shard_map/while/body/eval_jaxpr/nihd,njhd->nhij/dot_general | solution.py:90
  56.0 3.4 %multiply_reduce_fusion.1 = (f32[2,6,144]{2,1,0:T(8,128)S(1)}, f32[2,6,144,144]{2,3,1,0:T(8,128)}) fusion(f32[2,6,144,144]{2,3,1,0:T(8,128)S(1)} %fusion.29, f32[6,144,144]{1,2,0:T(8,128)} %copy.136, pred[144,144]{0,1:T(8,128)(4,1)S(1)} %copy-done.16, bf16[2,144,1,6,32]{1,0,4,3,2:T(2,128)(2,1)} %get-tuple-element.82, ...), kind=kOutput, calls=%fused_computation.5 | convolution fusion | flops 17418384 | bytes 2737152 | tf_op jit(solution)/shard_map/while/body/eval_jaxpr/div | solution.py:82
  59.4 2.0 %fusion.4 = bf16[2,144,1,6,32]{1,4,3,0,2:T(8,128)(2,1)S(1)} fusion(f32[2,6,144,144]{2,3,1,0:T(8,128)} %get-tuple-element.98, bf16[2,144,6,32]{1,0,3,2:T(2,128)(2,1)S(1)} %reshape.369), kind=kOutput, calls=%fused_computation.24 | convolution fusion | flops 16229376 | bytes 1216512 | tf_op jit(solution)/shard_map/while/body/eval_jaxpr/nhij,nihd->njhd/dot_general | solution.py:104
  61.4 1.3 %fusion.16 = (bf16[6,144,144]{1,2,0:T(8,128)(2,1)}, bf16[2,6,144,144]{2,3,1,0:T(8,128)(2,1)S(1)}) fusion(f32[2,6,144,144]{2,3,1,0:T(8,128)S(1)} %copy-done.2, f32[2,6,144,144]{2,3,1,0:T(8,128)S(1)} %fusion.29, f32[2,6,144]{2,1,0:T(8,128)S(1)} %get-tuple-element.97), kind=kLoop, calls=%fused_computation.38 | loop fusion | flops 870912 | bytes 2744064 | tf_op jit(solution)/shard_map/while/body/eval_jaxpr/reduce_sum | solution.py:93
  62.7 0.4 fusion.8
  63.1 0.3 fusion.9
  63.4 0.3 copy-done.5
  64.0 0.6 fusion.49
  64.7 0.3 pad_maximum_fusion.1
  65.0 1.1 %fusion.48 = (f32[2,144]{1,0:T(2,128)S(1)}, f32[2,144]{1,0:T(2,128)S(1)}, f32[2,144,192]{2,1,0:T(8,128)}) fusion(f32[2,144]{1,0:T(2,128)S(1)} %rsqrt.33, f32[2,144]{1,0:T(2,128)S(1)} %div.120, f32[2,144,192]{2,0,1:T(2,128)S(1)} %bitcast.122, f32[192]{0:T(256)S(1)} %copy-done.18, bf16[2,144,576]{1,2,0:T(8,128)(2,1)S(1)} %bitcast.125, ...), kind=kOutput, calls=%fused_computation.126 | convolution fusion | flops 64032192 | bytes 1000704 | tf_op jit(solution)/shard_map/while/body/eval_jaxpr/dot_general | solution.py:108
  66.2 0.5 copy.179
  66.7 0.5 copy.178
  67.2 0.3 maximum_bitcast_fusion
  67.5 1.8 %copy.180 = bf16[16,2,1,6,9,144]{5,1,4,3,2,0:T(2,128)(2,1)} copy(bf16[16,2,1,6,9,144]{5,3,4,0,2,1:T(8,128)(2,1)S(1)} %maximum_bitcast_fusion) | data formatting | bytes 995328 | tf_op jit(solution)/shard_map/transpose | solution.py:22
  69.4 6.9 %all-to-all-start = ((bf16[16,2,1,6,9,144]{5,1,4,3,2,0:T(2,128)(2,1)}), bf16[16,2,1,6,9,144]{5,1,4,3,2,0:T(2,128)(2,1)S(1)}, u32[]{:S(2)}, u32[]{:S(2)}) async-start(bf16[16,2,1,6,9,144]{5,1,4,3,2,0:T(2,128)(2,1)} %copy.180), calls=%async_computation | async-start | bytes 1769472 | tf_op jit(solution)/shard_map/all_to_all | solution.py:27
  76.2 0.2 multiply_convert_fusion
  76.6 0.2 multiply_convert_fusion.2
  76.9 0.5 maximum_bitcast_fusion.1
  77.4 0.2 copy.177
  77.6 0.3 reshape.373
  78.3 1.9 %collective-permute-start.2 = (bf16[4,3,24,192]{3,0,2,1:T(4,128)(2,1)S(1)}, bf16[4,3,24,192]{3,0,2,1:T(4,128)(2,1)S(1)}, u32[]{:S(2)}, u32[]{:S(2)}) collective-permute-start(bf16[4,3,24,192]{3,0,2,1:T(4,128)(2,1)S(1)} %fusion.34), channel_id=1, source_target_pairs={{0,16},{16,32},{32,48},{48,64},{64,80},{80,96},{96,112},{112,128},... | collective-permute-start | bytes 331784 | tf_op jit(solution)/shard_map/ppermute | solution.py:17
  80.2 9.5 %collective-permute-done.2 = bf16[4,3,24,192]{3,0,2,1:T(4,128)(2,1)S(1)} collective-permute-done((bf16[4,3,24,192]{3,0,2,1:T(4,128)(2,1)S(1)}, bf16[4,3,24,192]{3,0,2,1:T(4,128)(2,1)S(1)}, u32[]{:S(2)}, u32[]{:S(2)}) %collective-permute-start.2) | collective-permute-done | bytes 110624 | tf_op jit(solution)/shard_map/ppermute | solution.py:17
  89.8 2.3 %collective-permute-start.3 = (bf16[4,6,6,192]{3,0,2,1:T(4,128)(2,1)S(1)}, bf16[4,6,6,192]{3,0,2,1:T(4,128)(2,1)S(1)}, u32[]{:S(2)}, u32[]{:S(2)}) collective-permute-start(bf16[4,6,6,192]{3,0,2,1:T(4,128)(2,1)S(1)} %pad_maximum_fusion.7), channel_id=1, source_target_pairs={{0,1},{1,2},{2,3},{3,4},{4,5},{5,6},{6,7},{7,8},{8,9},{9,10},{10,1... | collective-permute-start | bytes 165896 | tf_op jit(solution)/shard_map/ppermute | solution.py:17
  92.1 6.0 %collective-permute-done.3 = bf16[4,6,6,192]{3,0,2,1:T(4,128)(2,1)S(1)} collective-permute-done((bf16[4,6,6,192]{3,0,2,1:T(4,128)(2,1)S(1)}, bf16[4,6,6,192]{3,0,2,1:T(4,128)(2,1)S(1)}, u32[]{:S(2)}, u32[]{:S(2)}) %collective-permute-start.3) | collective-permute-done | bytes 55328 | tf_op jit(solution)/shard_map/ppermute | solution.py:17
  98.2 0.2 fusion.23
  98.4 0.7 copy.184
  99.1 0.4 convert_reduce_fusion
  99.6 0.8 copy.185
  (85 shorter events, 4.2 us)
Async XLA Ops:
  0.6 35.5 %copy-start = (bf16[192,576]{1,0:T(8,128)(2,1)S(1)}, bf16[192,576]{1,0:T(8,128)(2,1)}, u32[]{:S(2)}) copy-start(bf16[192,576]{1,0:T(8,128)(2,1)} %param.9) | copy-start | bytes 663556
  1.9 21.4 %collective-permute-start = (bf16[2,4,3,24,192]{4,3,2,1,0:T(8,128)(2,1)S(1)}, bf16[2,4,3,24,192]{4,3,2,1,0:T(8,128)(2,1)S(1)}, u32[]{:S(2)}, u32[]{:S(2)}) collective-permute-start(bf16[2,4,3,24,192]{4,3,2,1,0:T(8,128)(2,1)S(1)} %get-tuple-element.89), channel_id=1, source_target_pairs={{0,752},{16,0},{32,16},{48,32},{64,48},{80,64},{96,80},{112,96},{1... | collective-permute-start | bytes 663560 | tf_op jit(solution)/shard_map/ppermute | solution.py:17
  23.3 9.4 %collective-permute-start.1 = (bf16[2,4,6,6,192]{4,3,2,1,0:T(8,128)(2,1)S(1)}, bf16[2,4,6,6,192]{4,3,2,1,0:T(8,128)(2,1)S(1)}, u32[]{:S(2)}, u32[]{:S(2)}) collective-permute-start(bf16[2,4,6,6,192]{4,3,2,1,0:T(8,128)(2,1)S(1)} %pad_maximum_fusion.6), channel_id=1, source_target_pairs={{0,15},{1,0},{2,1},{3,2},{4,3},{5,4},{6,5},{7,6},{8,7},{9,8},{10,9... | collective-permute-start | bytes 331784 | tf_op jit(solution)/shard_map/ppermute | solution.py:17
  34.4 1.7 %copy-start.18 = (f32[192]{0:T(256)S(1)}, f32[192]{0:T(256)}, u32[]{:S(2)}) copy-start(f32[192]{0:T(256)} %param.8) | copy-start | bytes 2308
  37.0 2.6 %copy-start.14 = (bf16[192,192]{1,0:T(8,128)(2,1)S(1)}, bf16[192,192]{1,0:T(8,128)(2,1)}, u32[]{:S(2)}) copy-start(bf16[192,192]{1,0:T(8,128)(2,1)} %param.10) | copy-start | bytes 221188
  39.4 2.0 %copy-start.8 = (bf16[2,144,1,6,32]{1,0,4,3,2:T(2,128)(2,1)S(1)}, bf16[2,144,1,6,32]{1,0,4,3,2:T(2,128)(2,1)}, u32[]{:S(2)}) copy-start(bf16[2,144,1,6,32]{1,0,4,3,2:T(2,128)(2,1)} %get-tuple-element.84) | copy-start | bytes 331780
  39.5 2.0 %copy-start.10 = (bf16[2,144,1,6,32]{1,0,4,3,2:T(2,128)(2,1)S(1)}, bf16[2,144,1,6,32]{1,0,4,3,2:T(2,128)(2,1)}, u32[]{:S(2)}) copy-start(bf16[2,144,1,6,32]{1,0,4,3,2:T(2,128)(2,1)} %get-tuple-element.85) | copy-start | bytes 331780
  45.3 2.7 %copy-start.1 = (f32[2,6,144,144]{2,3,1,0:T(8,128)S(1)}, f32[2,6,144,144]{2,3,1,0:T(8,128)}, u32[]{:S(2)}) copy-start(f32[2,6,144,144]{2,3,1,0:T(8,128)} %get-tuple-element.95) | copy-start | bytes 2985988
  45.3 2.7 %copy-start.17 = (f32[2,6,144]{2,1,0:T(8,128)S(1)}, f32[2,6,144]{2,1,0:T(8,128)}, u32[]{:S(2)}) copy-start(f32[2,6,144]{2,1,0:T(8,128)} %get-tuple-element.94) | copy-start | bytes 20740
  48.0 0.9 copy-start.11
  48.0 2.0 %copy-start.9 = (bf16[2,144,1,6,32]{1,0,4,3,2:T(2,128)(2,1)S(1)}, bf16[2,144,1,6,32]{1,0,4,3,2:T(2,128)(2,1)}, u32[]{:S(2)}) copy-start(bf16[2,144,1,6,32]{1,0,4,3,2:T(2,128)(2,1)} %get-tuple-element.84) | copy-start | bytes 331780
  51.9 2.1 %copy-start.13 = (bf16[1,1,2,2,6,12,192]{6,3,0,5,2,4,1:T(2,128)(2,1)S(1)}, bf16[1,1,2,2,6,12,192]{6,3,0,5,2,4,1:T(2,128)(2,1)}, u32[]{:S(2)}) copy-start(bf16[1,1,2,2,6,12,192]{6,3,0,5,2,4,1:T(2,128)(2,1)} %get-tuple-element.90) | copy-start | bytes 331780
  52.3 1.9 %copy-start.15 = (bf16[192,192]{1,0:T(8,128)(2,1)S(1)}, bf16[192,192]{1,0:T(8,128)(2,1)}, u32[]{:S(2)}) copy-start(bf16[192,192]{1,0:T(8,128)(2,1)} %param.10) | copy-start | bytes 221188
  54.0 2.0 %copy-start.16 = (pred[144,144]{0,1:T(8,128)(4,1)S(1)}, pred[144,144]{0,1:T(8,128)(4,1)}, u32[]{:S(2)}) copy-start(pred[144,144]{0,1:T(8,128)(4,1)} %broadcast_compare_fusion.1) | copy-start | bytes 62212
  59.4 2.0 %copy-start.2 = (f32[2,6,144,144]{2,3,1,0:T(8,128)S(1)}, f32[2,6,144,144]{2,3,1,0:T(8,128)}, u32[]{:S(2)}) copy-start(f32[2,6,144,144]{2,3,1,0:T(8,128)} %get-tuple-element.98) | copy-start | bytes 2985988
  61.4 1.3 %copy-start.12 = (bf16[2,144,1,6,32]{1,0,4,3,2:T(2,128)(2,1)S(1)}, bf16[2,144,1,6,32]{1,0,4,3,2:T(2,128)(2,1)}, u32[]{:S(2)}) copy-start(bf16[2,144,1,6,32]{1,0,4,3,2:T(2,128)(2,1)} %get-tuple-element.82) | copy-start | bytes 331780
  62.7 0.9 copy-start.5
  62.7 1.0 %copy-start.6 = (bf16[2,144,1,6,32]{1,4,3,0,2:T(8,128)(2,1)S(1)}, bf16[2,144,1,6,32]{1,4,3,0,2:T(8,128)(2,1)}, u32[]{:S(2)}) copy-start(bf16[2,144,1,6,32]{1,4,3,0,2:T(8,128)(2,1)} %fusion.6) | copy-start | bytes 331780
  62.7 1.1 %copy-start.7 = (bf16[2,144,1,6,32]{1,4,3,0,2:T(8,128)(2,1)S(1)}, bf16[2,144,1,6,32]{1,4,3,0,2:T(8,128)(2,1)}, u32[]{:S(2)}) copy-start(bf16[2,144,1,6,32]{1,4,3,0,2:T(8,128)(2,1)} %fusion.7) | copy-start | bytes 331780
  65.0 1.7 %copy-start.3 = (bf16[6,144,144]{1,2,0:T(8,128)(2,1)S(1)}, bf16[6,144,144]{1,2,0:T(8,128)(2,1)}, u32[]{:S(2)}) copy-start(bf16[6,144,144]{1,2,0:T(8,128)(2,1)} %get-tuple-element.64) | copy-start | bytes 746500
  69.4 7.2 %copy-start.4 = (f32[2,144,192]{2,1,0:T(8,128)S(1)}, f32[2,144,192]{2,1,0:T(8,128)}, u32[]{:S(2)}) copy-start(f32[2,144,192]{2,1,0:T(8,128)} %get-tuple-element.99) | copy-start | bytes 663556
  69.4 29.8 %all-to-all-start = ((bf16[16,2,1,6,9,144]{5,1,4,3,2,0:T(2,128)(2,1)}), bf16[16,2,1,6,9,144]{5,1,4,3,2,0:T(2,128)(2,1)S(1)}, u32[]{:S(2)}, u32[]{:S(2)}) async-start(bf16[16,2,1,6,9,144]{5,1,4,3,2,0:T(2,128)(2,1)} %copy.180), calls=%async_computation | async-start | bytes 1769472 | tf_op jit(solution)/shard_map/all_to_all | solution.py:27
  78.3 11.5 %collective-permute-start.2 = (bf16[4,3,24,192]{3,0,2,1:T(4,128)(2,1)S(1)}, bf16[4,3,24,192]{3,0,2,1:T(4,128)(2,1)S(1)}, u32[]{:S(2)}, u32[]{:S(2)}) collective-permute-start(bf16[4,3,24,192]{3,0,2,1:T(4,128)(2,1)S(1)} %fusion.34), channel_id=1, source_target_pairs={{0,16},{16,32},{32,48},{48,64},{64,80},{80,96},{96,112},{112,128},... | collective-permute-start | bytes 331784 | tf_op jit(solution)/shard_map/ppermute | solution.py:17
  89.8 8.4 %collective-permute-start.3 = (bf16[4,6,6,192]{3,0,2,1:T(4,128)(2,1)S(1)}, bf16[4,6,6,192]{3,0,2,1:T(4,128)(2,1)S(1)}, u32[]{:S(2)}, u32[]{:S(2)}) collective-permute-start(bf16[4,6,6,192]{3,0,2,1:T(4,128)(2,1)S(1)} %pad_maximum_fusion.7), channel_id=1, source_target_pairs={{0,1},{1,2},{2,3},{3,4},{4,5},{5,6},{6,7},{7,8},{8,9},{9,10},{10,1... | collective-permute-start | bytes 165896 | tf_op jit(solution)/shard_map/ppermute | solution.py:17
where the time goes:
time: 101 us; the launch traced here: 100 us
  starting transfers between devices  32.9 us (33%)
  matrix products  20.2 us (20%)
  waiting for transfers between devices  18.5 us (18%)
  local copies, waits for them, and re-layouts  18.4 us (18%)
  other arithmetic  9.06 us (9%)
  between operations  1.26 us (1%)
    ppermute x4, starting transfers between devices, from_behind(): lax.ppermute(value, axis, [(i, (i + by) % devices) for i in range(devices)])  26.1 us
    ppermute x4, waiting for transfers between devices, from_behind(): lax.ppermute(value, axis, [(i, (i + by) % devices) for i in range(devices)])  18.5 us
    div x2, matrix products, band_backward(): probabilities = weights / jnp.sum(weights, axis=-1, keepdims=True)  7.29 us
    all_to_all x1, starting transfers between devices, sum_at_owner(): lax.all_to_all(blocks, axis, split_axis=0, concat_axis=0, tiled=True)  6.85 us
    dot_general x2, matrix products, band_backward(): jnp.einsum('nhij,nihd->njhd', probs_low, upstream, preferred_element_type...  4.65 us
    add x3, local copies, waits for them, and re-layouts, band_backward(): jnp.einsum('nihd,njhd->nhij', query_rows, key_rows, preferred_element_typ...  4.3 us
    dot_general x2, matrix products, band_backward(): jnp.einsum('nihd,njhd->nhij', upstream, value_rows, preferred_element_typ...  2.74 us
    unnamed x41, local copies, waits for them, and re-layouts  2.56 us
  transfers between devices with their start and end apart: 5, of which 3 were waited for; matrix products, arithmetic and copies ran while one was open for 9% of the time, Pallas kernels for 0%

commit v1 on v0

v1 whole, which is shorter than its diff:
```python
import jax
import jax.numpy as jnp
from jax import lax
from jax.experimental import pallas as pl
from jax.experimental.pallas import tpu as pltpu
from jax.sharding import PartitionSpec as P

EPS = 1e-05
HEADS = 6
C = 192
LOG2E = 1.4426950408889634
SCALE = 32 ** (-0.5)
BF = jnp.bfloat16
F32 = jnp.float32
OWNERS = 16
LANES = 64 * OWNERS
GROUPS = ((1, 0, 2), (3, 2, 1), (0, 3, 1))
MESH = pl.DeviceIdType.MESH


def nn(a, b):
    return lax.dot_general(a, b, (((1,), (0,)), ((), ())), preferred_element_type=F32)


def nt(a, b):
    return lax.dot_general(a, b, (((1,), (1,)), ((), ())), preferred_element_type=F32)


def tn(a, b):
    return lax.dot_general(a, b, (((0,), (0,)), ((), ())), preferred_element_type=F32)


def iota(shape, dim):
    return lax.broadcasted_iota(jnp.int32, shape, dim)


def one_hot(cond):
    return jnp.where(cond, 1.0, 0.0).astype(BF)


def lane_head(shape):
    return ((iota(shape, 1) & 63) * 57) >> 9


def lane_query(shape):
    lane = iota(shape, 1)
    inner = lane & 63
    return 9 * (lane >> 6) + inner - 9 * ((inner * 57) >> 9)


def make_kernel(lat_count, lon_count):
    def kernel(
        tok, cot, gain_ref, win_ref, wout_ref, bias_ref, out_ref, bout_ref,
        x, bias_v, bt0, bt1, sel, mask, pc, pct, wq, wk, wv, wqt, wkt,
        ext, sb0, sb1, rb0, rb1, rl, rc, rd,
        bias_sem, own_sem, hs_sem, hr_sem, bs_sem, br_sem, gs_sem, gr_sem,
    ):
        lat = lax.axis_index("lat")
        lon = lax.axis_index("lon")
        lat_next = lax.rem(lat + 1, lat_count)
        lat_prev = lax.rem(lat + lat_count - 1, lat_count)
        lon_next = lax.rem(lon + 1, lon_count)
        lon_prev = lax.rem(lon + lon_count - 1, lon_count)

        barrier = pltpu.get_barrier_semaphore()

        def greet(r, carry):
            pl.semaphore_signal(
                barrier, inc=1, device_id=(lat, lax.rem(lon + r, lon_count)), device_id_type=MESH
            )
            return carry

        for there in ((lat_prev, lon), (lat_next, lon), (lat_prev, lon_prev), (lat_next, lon_next)):
            pl.semaphore_signal(barrier, inc=1, device_id=there, device_id_type=MESH)
        lax.fori_loop(1, lon_count, greet, 0)

        bias_copies = [
            pltpu.make_async_copy(bias_ref.at[a], bias_v.at[a], bias_sem.at[a]) for a in range(2)
        ]
        for copy in bias_copies:
            copy.start()
        own_copies = []
        for which, ref in enumerate((tok, cot)):
            for g, (src, z, count) in enumerate(GROUPS):
                own_copies.append(
                    pltpu.make_async_copy(
                        ref.at[src : src + count, 3:6],
                        x.at[which, z : z + count, 0:3, 0:3],
                        own_sem.at[which, g],
                    )
                )
                own_copies[-1].start()

        sel[...] = one_hot((iota((144, LANES), 0) == lane_query((144, LANES))) & (lane_head((144, LANES)) < HEADS))
        mask[...] = one_hot((iota((C, LANES), 0) >> 5) == lane_head((C, LANES)))
        for c in range(2):
            p = iota((72, 192), 0)
            row = (p * 43) >> 9
            pc[c] = one_hot(iota((72, 192), 1) == 32 * row + p - 12 * row + 6 + 12 * c)
            p = iota((192, 72), 1)
            row = (p * 43) >> 9
            pct[c] = one_hot(iota((192, 72), 0) == 32 * row + p - 12 * row + 6 + 12 * c)
        wq[...] = win_ref[:, 0:192]
        wk[...] = win_ref[:, 192:384]
        wv[...] = win_ref[:, 384:576]
        wqt[...] = wq[...].astype(F32).T.astype(BF)
        wkt[...] = wk[...].astype(F32).T.astype(BF)

        pl.semaphore_wait(barrier, lon_count - 1 + 4)

        halo_copies = [[], [], []]
        for g, (src, z, count) in enumerate(GROUPS):
            for which, ref in enumerate((tok, cot)):
                for kind, (source, target, there) in enumerate(
                    (
                        (ref.at[src : src + count, 0:3], x.at[which, z : z + count, 3:6, 0:3], (lat_prev, lon)),
                        (ref.at[src : src + count, 0:3, 0], x.at[which, z : z + count, 3:6, 3], (lat_prev, lon_prev)),
                        (ref.at[src : src + count, 3:6, 0], x.at[which, z : z + count, 0:3, 3], (lat, lon_prev)),
                    )
                ):
                    copy = pltpu.make_async_remote_copy(
                        src_ref=source,
                        dst_ref=target,
                        send_sem=hs_sem.at[which, kind, g],
                        recv_sem=hr_sem.at[which, kind, g],
                        device_id=there,
                        device_id_type=MESH,
                    )
                    copy.start()
                    halo_copies[g].append(copy)

        is_last = jnp.where(lat == lat_count - 1, -1e30, 0.0).astype(F32)

        def penalty(rows):
            key_late = lax.rem(iota((rows, 1), 0), 72) >= 36
            query_late = lax.rem(lane_query((1, 64 * rows // 9)), 72) >= 36
            return jnp.where(key_late != query_late, is_last, 0.0)

        for a in range(2):
            bias_copies[a].wait()
        heads0 = lane_head((1, LANES))
        total = jnp.zeros((144, LANES), F32)
        for h in range(HEADS):
            b = bias_v[0, 144 * h : 144 * h + 144, :] * LOG2E
            high = b.astype(BF)
            low = (b - high.astype(F32)).astype(BF)
            moved = tn(high, sel[...]) + tn(low, sel[...])
            total = jnp.where(heads0 == h, moved, total)
        bt0[...] = total + penalty(144)
        heads1 = lane_head((1, LANES // 2))
        for s in range(2):
            total = jnp.zeros((72, LANES // 2), F32)
            for h in range(HEADS):
                b = bias_v[1, 144 * h + 72 * s : 144 * h + 72 * s + 72, :] * LOG2E
                high = b.astype(BF)
                low = (b - high.astype(F32)).astype(BF)
                half = sel[0:72, 0 : LANES // 2]
                moved = (tn(high, half) + tn(low, half))[72 * s : 72 * s + 72]
                total = jnp.where(heads1 == h, moved, total)
            bt1[s] = total + penalty(72)

        gain = gain_ref[...]

        def segment(t, ct, biast, choose, block):
            centred = t - jnp.sum(t, axis=-1, keepdims=True) * (1.0 / C)
            inverse = lax.rsqrt(jnp.sum(centred * centred, axis=-1, keepdims=True) * (1.0 / C) + EPS)
            standard = centred * inverse
            normed = (standard * gain).astype(BF)
            qt = nt(wqt[...], normed).astype(BF)
            kt = nt(wkt[...], normed).astype(BF)
            k = nn(normed, wk[...]).astype(BF)
            v = nn(normed, wv[...]).astype(BF)
            ut = nt(wout_ref[...], ct).astype(BF)
            qbd = nn(qt, choose).astype(BF) * block
            ubd = nn(ut, choose).astype(BF) * block
            e = jnp.exp2(nn(k, qbd) * (SCALE * LOG2E) + biast)
            probs = e * (1.0 / jnp.sum(e, axis=0, keepdims=True))
            dprobs = nn(v, ubd)
            inner = jnp.sum(probs * dprobs, axis=0, keepdims=True)
            dscores = probs * (dprobs - inner)
            p_low = probs.astype(BF)
            d_low = dscores.astype(BF)
            dv = nt(p_low, ubd).astype(BF)
            dk = (nt(d_low, qbd) * SCALE).astype(BF)
            wide = (nn(kt, d_low) * SCALE).astype(BF) * block
            dq = nt(choose, wide).astype(BF)
            dnormed = nt(dq, wq[...]) + nt(dk, wk[...]) + nt(dv, wv[...])
            scaled = dnormed * gain
            grad = inverse * (
                scaled
                - jnp.sum(scaled, axis=-1, keepdims=True) * (1.0 / C)
                - standard * (jnp.sum(scaled * standard, axis=-1, keepdims=True) * (1.0 / C))
            )
            return grad, dscores

        lane = iota((1, 128), 1) < 64

        def load_level(which, z):
            return x[which, z].reshape(192, C)

        def store_level(z, parts):
            full = nn(pct[0], parts[0].astype(BF)) + nn(pct[1], parts[1].astype(BF))
            ext[z] = full.reshape(6, 4, 8, C).astype(BF)

        def send_grads(a):
            copies = []
            span = pl.ds(2 * a, 2)
            for kind, (source, target, there) in enumerate(
                (
                    (ext.at[span, 3:6, 0:3], rl.at[span], (lat_next, lon)),
                    (ext.at[span, 3:6, 3], rd.at[span], (lat_next, lon_next)),
                    (ext.at[span, 0:3, 3], rc.at[span], (lat, lon_next)),
                )
            ):
                copy = pltpu.make_async_remote_copy(
                    src_ref=source,
                    dst_ref=target,
                    send_sem=gs_sem.at[a, kind],
                    recv_sem=gr_sem.at[a, kind],
                    device_id=there,
                    device_id_type=MESH,
                )
                copy.start()
                copies.append(copy)
            return copies

        def bias_copy(a, r):
            there = lax.rem(lon + r, lon_count)
            source, target = ((sb0, rb0), (sb1, rb1))[a]
            return pltpu.make_async_remote_copy(
                src_ref=source.at[there],
                dst_ref=target.at[r],
                send_sem=bs_sem.at[a, r],
                recv_sem=br_sem.at[a, r],
                device_id=(lat, there),
                device_id_type=MESH,
            )

        def send_bias(a):
            def body(r, carry):
                bias_copy(a, r).start()
                return carry

            lax.fori_loop(1, lon_count, body, 0)

        for copy in own_copies:
            copy.wait()
        for copy in halo_copies[0]:
            copy.wait()

        grads = []
        db = None
        levels = [[load_level(which, z) for z in range(2)] for which in range(2)]
        for c in range(2):
            t = jnp.concatenate([nn(pc[c], levels[0][z]) for z in range(2)], axis=0)
            ct = jnp.concatenate([nn(pc[c], levels[1][z]) for z in range(2)], axis=0).astype(BF)
            grad, dscores = segment(t, ct, bt0[...], sel[...], mask[...])
            grads.append(grad)
            db = dscores if db is None else db + dscores
        for tile in range(OWNERS // 2):
            top = db[0:72, 128 * tile : 128 * tile + 128]
            bottom = db[72:144, 128 * tile : 128 * tile + 128]
            sb0[2 * tile] = jnp.where(lane, top, pltpu.roll(bottom, 64, 1)).astype(BF)
            sb0[2 * tile + 1] = jnp.where(lane, pltpu.roll(top, 64, 1), bottom).astype(BF)
        send_bias(0)
        for z in range(2):
            store_level(z, [grad[72 * z : 72 * z + 72] for grad in grads])
        grad_copies = send_grads(0)

        for g in (1, 2):
            for copy in halo_copies[g]:
                copy.wait()
        for s in range(2):
            tokens_here, cot_here = load_level(0, 2 + s), load_level(1, 2 + s)
            grads = []
            db = None
            for c in range(2):
                t = nn(pc[c], tokens_here)
                ct = nn(pc[c], cot_here).astype(BF)
                grad, dscores = segment(
                    t, ct, bt1[s], sel[0:72, 0 : LANES // 2], mask[:, 0 : LANES // 2]
                )
                grads.append(grad)
                db = dscores if db is None else db + dscores
            for tile in range(OWNERS // 4):
                part = db[:, 128 * tile : 128 * tile + 128]
                top, bottom = part[0:40], part[32:72]
                owner = OWNERS // 2 * s + 2 * tile
                sb1[owner] = jnp.where(lane, top, pltpu.roll(bottom, 64, 1)).astype(BF)
                sb1[owner + 1] = jnp.where(lane, pltpu.roll(top, 64, 1), bottom).astype(BF)
            store_level(2 + s, grads)
        send_bias(1)
        grad_copies += send_grads(1)

        for copy in grad_copies:
            copy.wait()
        for src, z, count in GROUPS:
            for i in range(count):
                out_ref[src + i, 0:3, 1:3] = rl[z + i, :, 1:3]
                out_ref[src + i, 0:3, 0] = rl[z + i, :, 0] + rd[z + i]
                out_ref[src + i, 3:6, 1:3] = ext[z + i, 0:3, 1:3]
                out_ref[src + i, 3:6, 0] = ext[z + i, 0:3, 0] + rc[z + i]

        def collect(r, carry):
            for a in range(2):
                bias_copy(a, r).wait()
            return carry[0] + rb0[r].astype(F32), carry[1] + rb1[r].astype(F32)

        sum0, sum1 = lax.fori_loop(
            1, lon_count, collect, (sb0[lon].astype(F32), sb1[lon].astype(F32))
        )
        first = jnp.concatenate([sum0, pltpu.roll(sum0, 64, 1)], axis=0)
        second = jnp.concatenate([pltpu.roll(sum1, 64, 1), sum1[8:40]], axis=0)
        early = lon < OWNERS // 2
        second = jnp.concatenate(
            [jnp.where(early, second, 0.0), jnp.where(early, 0.0, second)], axis=0
        )
        both = jnp.where(lane, first, second).T
        for a in range(2):
            for h in range(HEADS):
                bout_ref[a, h] = both[64 * a + 9 * h : 64 * a + 9 * h + 9]

    return kernel


def make_local(lat_count, lon_count):
    def local(tokens, cotangent, norm_gain, inproj_weight, outproj_weight, bias):
        any_spec = pl.BlockSpec(memory_space=pl.ANY)
        vmem = pl.BlockSpec(memory_space=pltpu.VMEM)
        dma = pltpu.SemaphoreType.DMA
        grad, bias_grad = pl.pallas_call(
            make_kernel(lat_count, lon_count),
            out_shape=(
                jax.ShapeDtypeStruct((4, 6, 3, 8, C), BF),
                jax.ShapeDtypeStruct((2, HEADS, 9, 144), F32),
            ),
            in_specs=[any_spec, any_spec, vmem, vmem, vmem, any_spec],
            out_specs=(vmem, vmem),
            scratch_shapes=[
                pltpu.VMEM((2, 4, 6, 4, 8, C), BF),
                pltpu.VMEM((2, 864, 144), F32),
                pltpu.VMEM((144, LANES), F32),
                pltpu.VMEM((2, 72, LANES // 2), F32),
                pltpu.VMEM((144, LANES), BF),
                pltpu.VMEM((C, LANES), BF),
                pltpu.VMEM((2, 72, 192), BF),
                pltpu.VMEM((2, 192, 72), BF),
                pltpu.VMEM((C, C), BF),
                pltpu.VMEM((C, C), BF),
                pltpu.VMEM((C, C), BF),
                pltpu.VMEM((C, C), BF),
                pltpu.VMEM((C, C), BF),
                pltpu.VMEM((4, 6, 4, 8, C), BF),
                pltpu.VMEM((OWNERS, 72, 128), BF),
                pltpu.VMEM((OWNERS, 40, 128), BF),
                pltpu.VMEM((OWNERS, 72, 128), BF),
                pltpu.VMEM((OWNERS, 40, 128), BF),
                pltpu.VMEM((4, 3, 3, 8, C), BF),
                pltpu.VMEM((4, 3, 8, C), BF),
                pltpu.VMEM((4, 3, 8, C), BF),
                dma((2,)),
                dma((2, 3)),
                dma((2, 3, 3)),
                dma((2, 3, 3)),
                dma((2, OWNERS)),
                dma((2, OWNERS)),
                dma((2, 3)),
                dma((2, 3)),
            ],
            compiler_params=pltpu.CompilerParams(collective_id=0, has_side_effects=True),
        )(
            tokens.reshape(4, 6, 3, 8, C),
            cotangent.reshape(4, 6, 3, 8, C),
            norm_gain.reshape(1, C),
            inproj_weight,
            outproj_weight,
            bias.reshape(2, 864, 144),
        )
        return grad.reshape(4, 6, 24, C), bias_grad.reshape(2, 1, HEADS, 9, 144)

    return local


def solution(mesh):
    placed = (
        P(None, "lat", "lon", None),
        P(None, "lat", "lon", None),
        P(),
        P(),
        P(),
        P(None, "lat", None, None, None),
    )
    return jax.shard_map(
        make_local(mesh.shape["lat"], mesh.shape["lon"]),
        mesh=mesh,
        in_specs=placed,
        out_specs=(P(None, "lat", "lon", None), P(None, "lat", None, "lon", None)),
        check_vma=False,
    )
```

time: 101 us -> 47.1 us (0.47)
  Pallas kernels: 0 us -> 42.9 us
  starting transfers between devices: 32.9 us -> 0 us
  matrix products: 20.2 us -> 0 us
  waiting for transfers between devices: 18.5 us -> 0 us
  local copies, waits for them, and re-layouts: 18.4 us -> 3.38 us
  other arithmetic: 9.06 us -> 0 us
    pallas_call x0 -> x1, Pallas kernels: none -> 42.9 us  [local(): pl.pallas_call(make_kernel(lat_count, lon_count), out_shape=(jax.ShapeDty...]
    ppermute x4 -> x0, starting transfers between devices: 26.1 us -> none  [from_behind(): lax.ppermute(value, axis, [(i, (i + by) % devices) for i in range(devices)])]
    ppermute x4 -> x0, waiting for transfers between devices: 18.5 us -> none  [from_behind(): lax.ppermute(value, axis, [(i, (i + by) % devices) for i in range(devices)])]
    dot_general x14 -> x0, matrix products: 12.9 us -> none  [the longest x2 4.65 us: band_backward(): jnp.einsum('nhij,nihd->njhd', probs_low, upstream, preferred_element_type...]
    div x2 -> x0, matrix products: 7.29 us -> none  [band_backward(): probabilities = weights / jnp.sum(weights, axis=-1, keepdims=True)]
    all_to_all x1 -> x0, starting transfers between devices: 6.85 us -> none  [sum_at_owner(): lax.all_to_all(blocks, axis, split_axis=0, concat_axis=0, tiled=True)]
    add x3 -> x0, local copies, waits for them, and re-layouts: 4.3 us -> none  [band_backward(): jnp.einsum('nihd,njhd->nhij', query_rows, key_rows, preferred_element_typ...]
    slice x9 -> x0, local copies, waits for them, and re-layouts: 3.88 us -> none  [the longest x2 2.47 us: band_backward(): value_rows = projected[:, :, 2]]
  transfers between devices with their start and end apart: 5 -> 0, of which waited for: 3 -> 0; matrix products, arithmetic and copies ran while one was open for 9% -> 0% of each run, Pallas kernels for 0% -> 0%
where the time goes in v1:
time: 47.1 us; the launch traced here: 46.9 us
  Pallas kernels  42.9 us (91%)
  local copies, waits for them, and re-layouts  3.38 us (7%)
  between operations  0.64 us (1%)
    pallas_call x1, Pallas kernels, local(): pl.pallas_call(make_kernel(lat_count, lon_count), out_shape=(jax.ShapeDty...  42.9 us
    unnamed x2, local copies, waits for them, and re-layouts  3.38 us

profile of v1, /device:TPU:2, one launch (start us, length us, event | category | flops | bytes accessed | tf_op | source)
XLA Modules:
  0.0 46.9 jit_solution(8691308765650330855)
XLA Ops:
  0.6 42.9 %shard_map.77 = (bf16[4,6,3,8,192]{4,3,2,1,0:T(8,128)(2,1)}, f32[2,6,9,144]{3,2,1,0:T(8,128)}) custom-call(bf16[4,6,3,8,192]{4,3,2,1,0:T(8,128)(2,1)} %bitcast.7, bf16[4,6,3,8,192]{4,3,2,1,0:T(8,128)(2,1)} %bitcast.8, f32[1,192]{1,0:T(1,128)} %bitcast.11, bf16[192,576]{1,0:T(8,128)(2,1)} %win_ref.1, bf16[192,192]{1,0:T(8,128)(2,1)} %wout_ref.1, ...), custom_call_target="tpu_custom_call" | custom-call | tf_op jit(solution)/shard_map/pallas_call | solution.py:331
  43.5 1.7 %copy.8 = f32[2,1,6,9,144]{4,1,3,2,0:T(1,128)} copy(f32[2,1,6,9,144]{4,3,2,0,1:T(8,128)} %bitcast.10) | data formatting | bytes 124416
  45.2 1.7 %copy.10 = bf16[4,6,24,192]{3,2,1,0:T(8,128)(2,1)} copy(bf16[4,6,24,192]{3,2,1,0:T(8,128)(2,1)} %bitcast.9) | data formatting | bytes 442368

commit v2 on v1

v2 whole, which is shorter than its diff:
```python
import jax
import jax.numpy as jnp
from jax import lax
from jax.experimental import pallas as pl
from jax.experimental.pallas import tpu as pltpu
from jax.sharding import PartitionSpec as P

EPS = 1e-05
HEADS = 6
C = 192
LOG2E = 1.4426950408889634
LN2 = 0.6931471805599453
SCALE = 32 ** (-0.5)
BF = jnp.bfloat16
F32 = jnp.float32
OWNERS = 16
HALF = 512
GROUPS = ((1, 0, 2), (3, 2, 1), (0, 3, 1))
MESH = pl.DeviceIdType.MESH


def nn(a, b):
    return lax.dot_general(a, b, (((1,), (0,)), ((), ())), preferred_element_type=F32)


def nt(a, b):
    return lax.dot_general(a, b, (((1,), (1,)), ((), ())), preferred_element_type=F32)


def tn(a, b):
    return lax.dot_general(a, b, (((0,), (0,)), ((), ())), preferred_element_type=F32)


def iota(shape, dim):
    return lax.broadcasted_iota(jnp.int32, shape, dim)


def one_hot(cond):
    return jnp.where(cond, 1.0, 0.0).astype(BF)


def lane_head():
    return ((iota((1, HALF), 1) & 63) * 57) >> 9


def lane_query():
    lane = iota((1, HALF), 1)
    return 9 * (lane >> 6) + (lane & 63) - 9 * lane_head()


def make_kernel(lat_count, lon_count):
    def kernel(
        tok, cot, gain_hbm, win_hbm, wout_hbm, bias_ref, rb0, rb1, gfull, edge,
        x, bias_v, bt0, bt1, perm, permb, choose, mask, pcs, pct,
        gain_ref, win_ref, wout_ref, wq, wk, wv, wqt, wkt,
        normed, standard, inverse, qbd, ubd, keys, vals, keyt, gq, gk, gv, ext, sb0, sb1,
        in_sem, own_sem, hs_sem, hr_sem, bs_sem, br_sem, gs_sem, gr_sem, keep_sem,
    ):
        lat = lax.axis_index("lat")
        lon = lax.axis_index("lon")
        half_count = lon_count // 2
        own_half = lon // half_count
        place = lax.rem(lon, half_count)
        other_half = 1 - own_half
        lat_next = lax.rem(lat + 1, lat_count)
        lat_prev = lax.rem(lat + lat_count - 1, lat_count)
        lon_next = lax.rem(lon + 1, lon_count)
        lon_prev = lax.rem(lon + lon_count - 1, lon_count)

        barrier = pltpu.get_barrier_semaphore()

        def greet(r, carry):
            pl.semaphore_signal(
                barrier, inc=1, device_id=(lat, lax.rem(lon + r, lon_count)), device_id_type=MESH
            )
            return carry

        for there in ((lat_prev, lon), (lat_next, lon), (lat_prev, lon_prev), (lat_next, lon_next)):
            pl.semaphore_signal(barrier, inc=1, device_id=there, device_id_type=MESH)
        lax.fori_loop(1, lon_count, greet, 0)

        own_copies = [[], [], []]
        for g, (src, z, count) in enumerate(GROUPS):
            for which, ref in enumerate((tok, cot)):
                copy = pltpu.make_async_copy(
                    ref.at[src : src + count, 3:6],
                    x.at[which, z : z + count, 0:3, 0:3],
                    own_sem.at[which, g],
                )
                copy.start()
                own_copies[g].append(copy)
        in_copies = [
            pltpu.make_async_copy(source, target, in_sem.at[i])
            for i, (source, target) in enumerate(
                (
                    (bias_ref.at[0], bias_v.at[0]),
                    (bias_ref.at[1], bias_v.at[1]),
                    (win_hbm, win_ref),
                    (wout_hbm, wout_ref),
                    (gain_hbm, gain_ref),
                )
            )
        ]
        for copy in in_copies:
            copy.start()

        pl.semaphore_wait(barrier, lon_count - 1 + 4)

        halo_copies = [[], [], []]
        for g, (src, z, count) in enumerate(GROUPS):
            for which, ref in enumerate((tok, cot)):
                for kind, (source, target, there) in enumerate(
                    (
                        (ref.at[src : src + count, 0:3, 0], x.at[which, z : z + count, 3:6, 3], (lat_prev, lon_prev)),
                        (ref.at[src : src + count, 3:6, 0], x.at[which, z : z + count, 0:3, 3], (lat, lon_prev)),
                        (ref.at[src : src + count, 0:3], x.at[which, z : z + count, 3:6, 0:3], (lat_prev, lon)),
                    )
                ):
                    copy = pltpu.make_async_remote_copy(
                        src_ref=source,
                        dst_ref=target,
                        send_sem=hs_sem.at[which, kind, g],
                        recv_sem=hr_sem.at[which, kind, g],
                        device_id=there,
                        device_id_type=MESH,
                    )
                    copy.start()
                    halo_copies[g].append(copy)

        heads, queries = lane_head(), lane_query()
        perm[...] = one_hot(iota((128 * HEADS, HALF), 0) == 128 * heads + queries)
        permb[...] = one_hot(iota((72 * HEADS, HALF), 0) == 72 * heads + queries)
        choose[...] = one_hot((iota((72, HALF), 0) == queries) & (heads < HEADS))
        mask[...] = one_hot((iota((C, HALF), 0) >> 5) == heads)
        for c in range(2):
            p = iota((72, 192), 0)
            row = (p * 43) >> 9
            pcs[c] = one_hot(iota((72, 192), 1) == 32 * row + p - 12 * row + 6 + 12 * c)
            p = iota((192, 72), 1)
            row = (p * 43) >> 9
            pct[c] = one_hot(iota((192, 72), 0) == 32 * row + p - 12 * row + 6 + 12 * c)
        for copy in in_copies:
            copy.wait()
        wq[...] = win_ref[:, 0:192]
        wk[...] = win_ref[:, 192:384]
        wv[...] = win_ref[:, 384:576]
        wqt[...] = wq[...].astype(F32).T.astype(BF)
        wkt[...] = wk[...].astype(F32).T.astype(BF)

        is_last = jnp.where(lat == lat_count - 1, -1e30, 0.0).astype(F32)
        query_late = queries >= 36

        def penalty(rows):
            return jnp.where((lax.rem(iota((rows, 1), 0), 72) >= 36) != query_late, is_last, 0.0)

        for a in range(2):
            for s in range(2):
                b = LOG2E * jnp.concatenate(
                    [bias_v[a, 144 * h + 72 * s : 144 * h + 72 * s + 72, :] for h in range(HEADS)], axis=0
                )
                high = b.astype(BF)
                low = (b - high.astype(F32)).astype(BF)
                moved = tn(high, permb[...]) + tn(low, permb[...])
                if a == 0:
                    bt0[s] = moved + penalty(144)
                else:
                    bt1[s] = moved[72 * s : 72 * s + 72] + penalty(72)

        gain = gain_ref[...]
        lane = iota((1, 128), 1) < 64
        blank = jnp.zeros((56, C), F32)

        def prepare(a):
            for l in range(2):
                t = nn(pcs[...].reshape(144, 192), x[0, 2 * a + l].reshape(192, C))
                centred = t - jnp.sum(t, axis=-1, keepdims=True) * (1.0 / C)
                inv = lax.rsqrt(jnp.sum(centred * centred, axis=-1, keepdims=True) * (1.0 / C) + EPS)
                unit = centred * inv
                inverse[l] = inv
                standard[l] = unit
                normed[l] = unit * gain
            compact = []
            for l in range(2):
                ct = nn(pcs[...].reshape(144, 192), x[1, 2 * a + l].reshape(192, C))
                for c in range(2):
                    rows = slice(72 * c, 72 * c + 72)
                    padded = jnp.concatenate([normed[l, rows], blank], axis=0).astype(BF)
                    qt = (nt(wqt[...], padded) * (SCALE * LOG2E)).astype(BF)
                    ut = nt(wout_ref[...], jnp.concatenate([ct[rows], blank], axis=0).astype(BF)).astype(BF)
                    for side in (qt, ut):
                        compact.append(
                            jnp.concatenate([side[32 * h : 32 * h + 32] for h in range(HEADS)], axis=1)
                        )
            wide = nn(jnp.concatenate(compact, axis=0), perm[...]).astype(BF)
            for l in range(2):
                for c in range(2):
                    at = 64 * (2 * l + c)
                    qbd[l, c] = jnp.concatenate([wide[at : at + 32]] * HEADS, axis=0) * mask[...]
                    ubd[l, c] = jnp.concatenate([wide[at + 32 : at + 64]] * HEADS, axis=0) * mask[...]

        def block(k, v, kt, s, c, biast):
            q, u = qbd[s, c], ubd[s, c]
            e = jnp.exp2(nn(k, q) + biast)
            probs = e * (1.0 / jnp.sum(e, axis=0, keepdims=True))
            weighted = probs * nn(v, u)
            dscores = weighted - probs * jnp.sum(weighted, axis=0, keepdims=True)
            low = dscores.astype(BF)
            dv = nt(probs.astype(BF), u)
            dk = nt(low, q) * LN2
            gq[s, c] = nt(choose[...], nn(kt, low).astype(BF) * mask[...])
            return dk, dv, dscores

        def finish(a):
            dq, dk, dv = (ref[...].reshape(288, C).astype(BF) for ref in (gq, gk, gv))
            scaled = (nt(dq, wq[...]) + nt(dk, wk[...]) + nt(dv, wv[...])) * gain
            for l in range(2):
                part = scaled[144 * l : 144 * l + 144]
                unit = standard[l]
                grad = inverse[l] * (
                    part
                    - jnp.sum(part, axis=-1, keepdims=True) * (1.0 / C)
                    - unit * (jnp.sum(part * unit, axis=-1, keepdims=True) * (1.0 / C))
                )
                full = nn(pct[0], grad[0:72].astype(BF)) + nn(pct[1], grad[72:144].astype(BF))
                ext[(2 * a + l + 1) % 4] = full.reshape(6, 4, 8, C).astype(BF)

        def send_grads(groups):
            copies = []
            for g in groups:
                level, _, count = GROUPS[g]
                span = pl.ds(level, count)
                for kind, (source, target, there) in enumerate(
                    (
                        (ext.at[span, 3:6, 3], edge.at[span, 0:3], (lat_next, lon_next)),
                        (ext.at[span, 0:3, 3], edge.at[span, 3:6], (lat, lon_next)),
                        (ext.at[span, 3:6, 0:3], gfull.at[span, 0:3], (lat_next, lon)),
                    )
                ):
                    copies.append(
                        pltpu.make_async_remote_copy(
                            src_ref=source,
                            dst_ref=target,
                            send_sem=gs_sem.at[g, kind],
                            recv_sem=gr_sem.at[g, kind],
                            device_id=there,
                            device_id_type=MESH,
                        )
                    )
                copies.append(
                    pltpu.make_async_copy(
                        ext.at[span, 0:3, 0:3], gfull.at[span, 3:6], keep_sem.at[g]
                    )
                )
            for copy in copies:
                copy.start()
            return copies

        def bias_copy(a, slot):
            half = jnp.where(slot >= half_count, other_half, own_half)
            there = half_count * half + lax.rem(place + slot, half_count)
            source, target = ((sb0, rb0), (sb1, rb1))[a]
            return pltpu.make_async_remote_copy(
                src_ref=source.at[there],
                dst_ref=target.at[slot],
                send_sem=bs_sem.at[a, slot],
                recv_sem=br_sem.at[a, slot],
                device_id=(lat, there),
                device_id_type=MESH,
            )

        def keep_copy(a):
            source, target = ((sb0, rb0), (sb1, rb1))[a]
            return pltpu.make_async_copy(source.at[lon], target.at[0], keep_sem.at[3 + a])

        def send_bias(a, i):
            def body(slot, carry):
                bias_copy(a, slot).start()
                return carry

            if i == 0:
                lax.fori_loop(half_count, lon_count, body, 0)
            else:
                lax.fori_loop(1, half_count, body, 0)
                keep_copy(a).start()

        def arrived(g):
            for copy in own_copies[g] + halo_copies[g]:
                copy.wait()

        arrived(0)
        prepare(0)
        for c in range(2):
            whole = jnp.concatenate([normed[l, 72 * c : 72 * c + 72] for l in range(2)], axis=0).astype(BF)
            keys[c] = nn(whole, wk[...]).astype(BF)
            vals[c] = nn(whole, wv[...]).astype(BF)
            keyt[c] = (nt(wkt[...], whole) * SCALE).astype(BF)
        totals = [None, None]
        for i, s in enumerate((other_half, own_half)):
            db = None
            for c in range(2):
                dk, dv, dscores = block(keys[c], vals[c], keyt[c], s, c, bt0[s])
                db = dscores if db is None else db + dscores
                totals[c] = (dk, dv) if i == 0 else (totals[c][0] + dk, totals[c][1] + dv)
            for tile in range(4):
                top = db[0:72, 128 * tile : 128 * tile + 128]
                bottom = db[72:144, 128 * tile : 128 * tile + 128]
                owner = half_count * s + 2 * tile
                sb0[owner] = jnp.where(lane, top, pltpu.roll(bottom, 64, 1)).astype(BF)
                sb0[owner + 1] = jnp.where(lane, pltpu.roll(top, 64, 1), bottom).astype(BF)
            send_bias(0, i)
        for c in range(2):
            for l in range(2):
                gk[l, c] = totals[c][0][72 * l : 72 * l + 72]
                gv[l, c] = totals[c][1][72 * l : 72 * l + 72]
        finish(0)
        grad_copies = send_grads((0,))

        arrived(1)
        arrived(2)
        prepare(1)
        for l in range(2):
            for c in range(2):
                part = normed[l, 72 * c : 72 * c + 72].astype(BF)
                keys[2 + 2 * l + c, 0:72] = nn(part, wk[...]).astype(BF)
                vals[2 + 2 * l + c, 0:72] = nn(part, wv[...]).astype(BF)
                keyt[2 + 2 * l + c, :, 0:72] = (nt(wkt[...], part) * SCALE).astype(BF)
        for i, s in enumerate((other_half, own_half)):
            db = None
            for c in range(2):
                at = 2 + 2 * s + c
                dk, dv, dscores = block(
                    keys[at, 0:72], vals[at, 0:72], keyt[at, :, 0:72], s, c, bt1[s]
                )
                gk[s, c] = dk
                gv[s, c] = dv
                db = dscores if db is None else db + dscores
            for tile in range(4):
                part = db[:, 128 * tile : 128 * tile + 128]
                top, bottom = part[0:40], part[32:72]
                owner = half_count * s + 2 * tile
                sb1[owner] = jnp.where(lane, top, pltpu.roll(bottom, 64, 1)).astype(BF)
                sb1[owner + 1] = jnp.where(lane, pltpu.roll(top, 64, 1), bottom).astype(BF)
            send_bias(1, i)
        finish(1)
        grad_copies += send_grads((1, 2))

        for copy in grad_copies:
            copy.wait()
        for a in range(2):
            keep_copy(a).wait()

        def collect(slot, carry):
            for a in range(2):
                bias_copy(a, slot).wait()
            return carry

        lax.fori_loop(1, lon_count, collect, 0)

    return kernel


def make_final(lon_count):
    def final(rb0, rb1, gfull, edge, out_ref, bout_ref):
        lane = iota((1, 128), 1) < 64
        out_ref[:, :, 1:3] = gfull[:, :, 1:3]
        out_ref[:, :, 0] = gfull[:, :, 0] + edge[...]
        sum0, sum1 = rb0[0].astype(F32), rb1[0].astype(F32)
        for slot in range(1, lon_count):
            sum0 += rb0[slot].astype(F32)
            sum1 += rb1[slot].astype(F32)
        first = jnp.concatenate([sum0, pltpu.roll(sum0, 64, 1)], axis=0)
        second = jnp.concatenate([pltpu.roll(sum1, 64, 1), sum1[8:40]], axis=0)
        early = lax.axis_index("lon") < lon_count // 2
        second = jnp.concatenate(
            [jnp.where(early, second, 0.0), jnp.where(early, 0.0, second)], axis=0
        )
        both = jnp.where(lane, first, second).T
        for a in range(2):
            for h in range(HEADS):
                for q in range(9):
                    at = 64 * a + 9 * h + q
                    bout_ref[a, h, q] = both[at : at + 1]

    return final


def make_local(lat_count, lon_count):
    def local(tokens, cotangent, norm_gain, inproj_weight, outproj_weight, bias):
        any_spec = pl.BlockSpec(memory_space=pl.ANY)
        vmem = pl.BlockSpec(memory_space=pltpu.VMEM)
        dma = pltpu.SemaphoreType.DMA
        parts = pl.pallas_call(
            make_kernel(lat_count, lon_count),
            out_shape=(
                jax.ShapeDtypeStruct((OWNERS, 72, 128), BF),
                jax.ShapeDtypeStruct((OWNERS, 40, 128), BF),
                jax.ShapeDtypeStruct((4, 6, 3, 8, C), BF),
                jax.ShapeDtypeStruct((4, 6, 8, C), BF),
            ),
            in_specs=[any_spec] * 6,
            out_specs=(any_spec,) * 4,
            scratch_shapes=[
                pltpu.VMEM((2, 4, 6, 4, 8, C), BF),
                pltpu.VMEM((2, 864, 144), F32),
                pltpu.VMEM((2, 144, HALF), F32),
                pltpu.VMEM((2, 72, HALF), F32),
                pltpu.VMEM((128 * HEADS, HALF), BF),
                pltpu.VMEM((72 * HEADS, HALF), BF),
                pltpu.VMEM((72, HALF), BF),
                pltpu.VMEM((C, HALF), BF),
                pltpu.VMEM((2, 72, 192), BF),
                pltpu.VMEM((2, 192, 72), BF),
                pltpu.VMEM((1, C), F32),
                pltpu.VMEM((C, 3 * C), BF),
                pltpu.VMEM((C, C), BF),
            ]
            + [pltpu.VMEM((C, C), BF)] * 5
            + [
                pltpu.VMEM((2, 144, C), F32),
                pltpu.VMEM((2, 144, C), F32),
                pltpu.VMEM((2, 144, 1), F32),
                pltpu.VMEM((2, 2, C, HALF), BF),
                pltpu.VMEM((2, 2, C, HALF), BF),
                pltpu.VMEM((6, 144, C), BF),
                pltpu.VMEM((6, 144, C), BF),
                pltpu.VMEM((6, C, 144), BF),
                pltpu.VMEM((2, 2, 72, C), F32),
                pltpu.VMEM((2, 2, 72, C), F32),
                pltpu.VMEM((2, 2, 72, C), F32),
                pltpu.VMEM((4, 6, 4, 8, C), BF),
                pltpu.VMEM((OWNERS, 72, 128), BF),
                pltpu.VMEM((OWNERS, 40, 128), BF),
                dma((5,)),
                dma((2, 3)),
                dma((2, 3, 3)),
                dma((2, 3, 3)),
                dma((2, OWNERS)),
                dma((2, OWNERS)),
                dma((3, 3)),
                dma((3, 3)),
                dma((5,)),
            ],
            compiler_params=pltpu.CompilerParams(collective_id=0, has_side_effects=True),
        )(
            tokens.reshape(4, 6, 3, 8, C),
            cotangent.reshape(4, 6, 3, 8, C),
            norm_gain.reshape(1, C),
            inproj_weight,
            outproj_weight,
            bias.reshape(2, 864, 144),
        )
        grad, bias_grad = pl.pallas_call(
            make_final(lon_count),
            out_shape=(
                jax.ShapeDtypeStruct((4, 6, 3, 8, C), BF),
                jax.ShapeDtypeStruct((2, HEADS, 9, 1, 144), F32),
            ),
            in_specs=[vmem] * 4,
            out_specs=(vmem, vmem),
        )(*parts)
        return grad.reshape(4, 6, 24, C), bias_grad.reshape(2, 1, HEADS, 9, 144)

    return local


def solution(mesh):
    placed = (
        P(None, "lat", "lon", None),
        P(None, "lat", "lon", None),
        P(),
        P(),
        P(),
        P(None, "lat", None, None, None),
    )
    return jax.shard_map(
        make_local(mesh.shape["lat"], mesh.shape["lon"]),
        mesh=mesh,
        in_specs=placed,
        out_specs=(P(None, "lat", "lon", None), P(None, "lat", None, "lon", None)),
        check_vma=False,
    )
```

time: 47.1 us -> 42.9 us (0.911)
  local copies, waits for them, and re-layouts: 3.38 us -> 0 us
  Pallas kernels: 42.9 us -> 42.1 us
    unnamed x2 -> x0, local copies, waits for them, and re-layouts: 3.38 us -> none
    pallas_call x1, Pallas kernels: 42.9 us -> 40.1 us  [local(): pl.pallas_call(make_kernel(lat_count, lon_count), out_shape=(jax.ShapeDty...]
    pallas_call x0 -> x1, Pallas kernels: none -> 2.04 us  [local(): pl.pallas_call(make_final(lon_count), out_shape=(jax.ShapeDtypeStruct((4,...]
where the time goes in v2:
time: 42.9 us; the launch traced here: 42.8 us
  Pallas kernels  42.1 us (98%)
  between operations  0.64 us (1%)
    pallas_call x1, Pallas kernels, local(): pl.pallas_call(make_kernel(lat_count, lon_count), out_shape=(jax.ShapeDty...  40.1 us
    pallas_call x1, Pallas kernels, local(): pl.pallas_call(make_final(lon_count), out_shape=(jax.ShapeDtypeStruct((4,...  2.04 us

profile of v2, /device:TPU:2, one launch (start us, length us, event | category | flops | bytes accessed | tf_op | source)
XLA Modules:
  0.0 42.8 jit_solution(12687703048716305064)
XLA Ops:
  0.6 40.1 %shard_map.77 = (bf16[16,72,128]{2,1,0:T(8,128)(2,1)}, bf16[16,40,128]{2,1,0:T(8,128)(2,1)}, bf16[4,6,3,8,192]{4,3,2,1,0:T(8,128)(2,1)}, bf16[4,6,8,192]{3,2,1,0:T(8,128)(2,1)}) custom-call(bf16[4,6,3,8,192]{4,3,2,1,0:T(8,128)(2,1)} %bitcast.7, bf16[4,6,3,8,192]{4,3,2,1,0:T(8,128)(2,1)} %bitcast.8, f32[1,192]{1,0:T(1,128)} %bitcast.9, ...), custom_call_target="tpu_custom_call" | custom-call | tf_op jit(solution)/shard_map/pallas_call | solution.py:392
  40.7 2.0 %shard_map.78 = (bf16[4,6,3,8,192]{4,3,2,1,0:T(8,128)(2,1)}, f32[2,6,9,1,144]{4,3,2,1,0:T(1,128)}) custom-call(bf16[16,72,128]{2,1,0:T(8,128)(2,1)} %get-tuple-element.8.rb0, bf16[16,40,128]{2,1,0:T(8,128)(2,1)} %get-tuple-element.9.rb1, bf16[4,6,3,8,192]{4,3,2,1,0:T(8,128)(2,1)} %get-tuple-element.10.gfull, bf16[4,6,8,192]{3,2,1,0:T(8,128)(2,1)} %get-tuple-element.11.edge), custom_call_target="tpu_custom_call" | custom-call | tf_op jit(solution)/shard_map/pallas_call | solution.py:452

commit v3 on v2

--- a/solution.py
+++ b/solution.py
@@ -52,8 +52,8 @@
     def kernel(
         tok, cot, gain_hbm, win_hbm, wout_hbm, bias_ref, rb0, rb1, gfull, edge,
         x, bias_v, bt0, bt1, perm, permb, choose, mask, pcs, pct,
-        gain_ref, win_ref, wout_ref, wq, wk, wv, wqt, wkt,
-        normed, standard, inverse, qbd, ubd, keys, vals, keyt, gq, gk, gv, ext, sb0, sb1,
+        gain_ref, win_ref, wout_ref, wq, wk, wv, wqkt,
+        standard, inverse, qbd, ubd, keys, vals, keyt, gq, gk, gv, ext, sb0, sb1,
         in_sem, own_sem, hs_sem, hr_sem, bs_sem, br_sem, gs_sem, gr_sem, keep_sem,
     ):
         lat = lax.axis_index("lat")
@@ -132,20 +132,21 @@
         permb[...] = one_hot(iota((72 * HEADS, HALF), 0) == 72 * heads + queries)
         choose[...] = one_hot((iota((72, HALF), 0) == queries) & (heads < HEADS))
         mask[...] = one_hot((iota((C, HALF), 0) >> 5) == heads)
-        for c in range(2):
-            p = iota((72, 192), 0)
-            row = (p * 43) >> 9
-            pcs[c] = one_hot(iota((72, 192), 1) == 32 * row + p - 12 * row + 6 + 12 * c)
-            p = iota((192, 72), 1)
-            row = (p * 43) >> 9
-            pct[c] = one_hot(iota((192, 72), 0) == 32 * row + p - 12 * row + 6 + 12 * c)
+        def grid_place(token):
+            c = (token >= 72).astype(jnp.int32)
+            inside = token - 72 * c
+            row = (inside * 43) >> 9
+            return 32 * row + inside - 12 * row + 6 + 12 * c
+
+        pcs[...] = one_hot(iota((144, 192), 1) == grid_place(iota((144, 192), 0)))
+        pct[...] = one_hot(iota((192, 144), 0) == grid_place(iota((192, 144), 1)))
         for copy in in_copies:
             copy.wait()
         wq[...] = win_ref[:, 0:192]
         wk[...] = win_ref[:, 192:384]
         wv[...] = win_ref[:, 384:576]
-        wqt[...] = wq[...].astype(F32).T.astype(BF)
-        wkt[...] = wk[...].astype(F32).T.astype(BF)
+        wqkt[0:192] = wq[...].astype(F32).T.astype(BF)
+        wqkt[192:384] = wk[...].astype(F32).T.astype(BF)
 
         is_last = jnp.where(lat == lat_count - 1, -1e30, 0.0).astype(F32)
         query_late = queries >= 36
@@ -170,59 +171,129 @@
         lane = iota((1, 128), 1) < 64
         blank = jnp.zeros((56, C), F32)
 
+        def pad_pair(v):
+            return jnp.concatenate([v[0:72], blank, v[72:144], blank], axis=0).astype(BF)
+
+        def compact(sides):
+            return jnp.concatenate(
+                [
+                    jnp.concatenate(
+                        [side[32 * h : 32 * h + 32, 128 * c : 128 * c + 128] for h in range(HEADS)], axis=1
+                    )
+                    for side in sides
+                    for c in range(2)
+                ],
+                axis=0,
+            )
+
+        def expand(target, wide):
+            for l in range(2):
+                for c in range(2):
+                    at = 32 * (2 * l + c)
+                    target[l, c] = jnp.concatenate([wide[at : at + 32]] * HEADS, axis=0) * mask[...]
+
         def prepare(a):
+            ts = [nn(pcs[...], x[0, 2 * a + l].reshape(192, C)) for l in range(2)]
+            cts = [nn(pcs[...], x[1, 2 * a + l].reshape(192, C)) for l in range(2)]
+            yield
+            uts = [nt(wout_ref[...], pad_pair(cts[l])).astype(BF) for l in range(2)]
+            plain = []
             for l in range(2):
-                t = nn(pcs[...].reshape(144, 192), x[0, 2 * a + l].reshape(192, C))
-                centred = t - jnp.sum(t, axis=-1, keepdims=True) * (1.0 / C)
+                centred = ts[l] - jnp.sum(ts[l], axis=-1, keepdims=True) * (1.0 / C)
                 inv = lax.rsqrt(jnp.sum(centred * centred, axis=-1, keepdims=True) * (1.0 / C) + EPS)
                 unit = centred * inv
-                inverse[l] = inv
-                standard[l] = unit
-                normed[l] = unit * gain
-            compact = []
+                inverse[a, l] = inv
+                standard[a, l] = unit
+                plain.append(unit * gain)
+            yield
+            expand(ubd.at[a], nn(compact(uts), perm[...]).astype(BF))
+            yield
+            qts = []
             for l in range(2):
-                ct = nn(pcs[...].reshape(144, 192), x[1, 2 * a + l].reshape(192, C))
+                projected = nt(wqkt[...] if a else wqkt[0:192], pad_pair(plain[l]))
+                qts.append((projected[0:192] * (SCALE * LOG2E)).astype(BF))
+                if a:
+                    for c in range(2):
+                        keyt[2 + 2 * l + c, :, 0:72] = (
+                            projected[192:384, 128 * c : 128 * c + 72] * SCALE
+                        ).astype(BF)
+            yield
+            together = jnp.concatenate(plain, axis=0).astype(BF)
+            for target, weight in ((keys, wk), (vals, wv)):
+                rows = nn(together, weight[...])
                 for c in range(2):
-                    rows = slice(72 * c, 72 * c + 72)
-                    padded = jnp.concatenate([normed[l, rows], blank], axis=0).astype(BF)
-                    qt = (nt(wqt[...], padded) * (SCALE * LOG2E)).astype(BF)
-                    ut = nt(wout_ref[...], jnp.concatenate([ct[rows], blank], axis=0).astype(BF)).astype(BF)
-                    for side in (qt, ut):
-                        compact.append(
-                            jnp.concatenate([side[32 * h : 32 * h + 32] for h in range(HEADS)], axis=1)
-                        )
-            wide = nn(jnp.concatenate(compact, axis=0), perm[...]).astype(BF)
-            for l in range(2):
+                    if a:
+                        for l in range(2):
+                            at = 144 * l + 72 * c
+                            target[2 + 2 * l + c, 0:72] = rows[at : at + 72].astype(BF)
+                    else:
+                        target[c] = jnp.concatenate(
+                            [rows[72 * c : 72 * c + 72], rows[144 + 72 * c : 216 + 72 * c]], axis=0
+                        ).astype(BF)
+            if not a:
                 for c in range(2):
-                    at = 64 * (2 * l + c)
-                    qbd[l, c] = jnp.concatenate([wide[at : at + 32]] * HEADS, axis=0) * mask[...]
-                    ubd[l, c] = jnp.concatenate([wide[at + 32 : at + 64]] * HEADS, axis=0) * mask[...]
-
-        def block(k, v, kt, s, c, biast):
-            q, u = qbd[s, c], ubd[s, c]
-            e = jnp.exp2(nn(k, q) + biast)
+                    whole = jnp.concatenate([v[72 * c : 72 * c + 72] for v in plain], axis=0).astype(BF)
+                    keyt[c] = (nt(wqkt[192:384], whole) * SCALE).astype(BF)
+            yield
+            expand(qbd.at[a], nn(compact(qts), perm[...]).astype(BF))
+            yield
+
+        sums = {}
+        parts = {}
+
+        def block(a, s, c):
+            if a:
+                at = 2 + 2 * s + c
+                k, v, kt, biast = keys[at, 0:72], vals[at, 0:72], keyt[at, :, 0:72], bt1[s]
+            else:
+                k, v, kt, biast = keys[c], vals[c], keyt[c], bt0[s]
+            scores = nn(k, qbd[a, s, c])
+            dprobs = nn(v, ubd[a, s, c])
+            yield
+            e = jnp.exp2(scores + biast)
             probs = e * (1.0 / jnp.sum(e, axis=0, keepdims=True))
-            weighted = probs * nn(v, u)
+            weighted = probs * dprobs
             dscores = weighted - probs * jnp.sum(weighted, axis=0, keepdims=True)
+            sums[a, s] = dscores if c == 0 else sums[a, s] + dscores
             low = dscores.astype(BF)
-            dv = nt(probs.astype(BF), u)
-            dk = nt(low, q) * LN2
-            gq[s, c] = nt(choose[...], nn(kt, low).astype(BF) * mask[...])
-            return dk, dv, dscores
+            dv = nt(probs.astype(BF), ubd[a, s, c])
+            wide = nn(kt, low)
+            dk = nt(low, qbd[a, s, c]) * LN2
+            if a:
+                gk[a, s, c] = dk
+                gv[a, s, c] = dv
+            elif s == 0:
+                parts[c] = (dk, dv)
+            else:
+                for target, total in ((gk, parts[c][0] + dk), (gv, parts[c][1] + dv)):
+                    for l in range(2):
+                        target[a, l, c] = total[72 * l : 72 * l + 72]
+            yield
+            gq[a, s, c] = nt(choose[...], wide.astype(BF) * mask[...])
+            yield
+
+        def pack(a, s):
+            for tile in range(4):
+                part = sums[a, s][:, 128 * tile : 128 * tile + 128]
+                target, top, bottom = (sb1, part[0:40], part[32:72]) if a else (sb0, part[0:72], part[72:144])
+                owner = 8 * s + 2 * tile
+                target[owner] = jnp.where(lane, top, pltpu.roll(bottom, 64, 1)).astype(BF)
+                target[owner + 1] = jnp.where(lane, pltpu.roll(top, 64, 1), bottom).astype(BF)
 
         def finish(a):
-            dq, dk, dv = (ref[...].reshape(288, C).astype(BF) for ref in (gq, gk, gv))
+            dq, dk, dv = (ref[a].reshape(288, C).astype(BF) for ref in (gq, gk, gv))
             scaled = (nt(dq, wq[...]) + nt(dk, wk[...]) + nt(dv, wv[...])) * gain
+            yield
             for l in range(2):
                 part = scaled[144 * l : 144 * l + 144]
-                unit = standard[l]
-                grad = inverse[l] * (
+                unit = standard[a, l]
+                grad = inverse[a, l] * (
                     part
                     - jnp.sum(part, axis=-1, keepdims=True) * (1.0 / C)
                     - unit * (jnp.sum(part * unit, axis=-1, keepdims=True) * (1.0 / C))
                 )
-                full = nn(pct[0], grad[0:72].astype(BF)) + nn(pct[1], grad[72:144].astype(BF))
-                ext[(2 * a + l + 1) % 4] = full.reshape(6, 4, 8, C).astype(BF)
+                ext[(2 * a + l + 1) % 4] = nn(pct[...], grad.astype(BF)).reshape(6, 4, 8, C).astype(BF)
+            yield
 
         def send_grads(groups):
             copies = []
@@ -256,8 +327,8 @@
             return copies
 
         def bias_copy(a, slot):
-            half = jnp.where(slot >= half_count, other_half, own_half)
-            there = half_count * half + lax.rem(place + slot, half_count)
+            half = other_half if slot >= half_count else own_half
+            there = half_count * half + ((place + slot) & (half_count - 1))
             source, target = ((sb0, rb0), (sb1, rb1))[a]
             return pltpu.make_async_remote_copy(
                 src_ref=source.at[there],
@@ -272,89 +343,49 @@
             source, target = ((sb0, rb0), (sb1, rb1))[a]
             return pltpu.make_async_copy(source.at[lon], target.at[0], keep_sem.at[3 + a])
 
-        def send_bias(a, i):
-            def body(slot, carry):
+        def send_bias(a):
+            for slot in range(half_count, lon_count):
                 bias_copy(a, slot).start()
-                return carry
-
-            if i == 0:
-                lax.fori_loop(half_count, lon_count, body, 0)
-            else:
-                lax.fori_loop(1, half_count, body, 0)
-                keep_copy(a).start()
+            for slot in range(1, half_count):
+                bias_copy(a, slot).start()
+            keep_copy(a).start()
 
         def arrived(g):
             for copy in own_copies[g] + halo_copies[g]:
                 copy.wait()
 
+        def run(*pieces):
+            for piece in pieces:
+                next(piece)
+
+        p0, p1, f0, f1 = prepare(0), prepare(1), finish(0), finish(1)
+        b0, b1, b2, b3 = (block(0, s, c) for s in range(2) for c in range(2))
+        b4, b5, b6, b7 = (block(1, s, c) for s in range(2) for c in range(2))
         arrived(0)
-        prepare(0)
-        for c in range(2):
-            whole = jnp.concatenate([normed[l, 72 * c : 72 * c + 72] for l in range(2)], axis=0).astype(BF)
-            keys[c] = nn(whole, wk[...]).astype(BF)
-            vals[c] = nn(whole, wv[...]).astype(BF)
-            keyt[c] = (nt(wkt[...], whole) * SCALE).astype(BF)
-        totals = [None, None]
-        for i, s in enumerate((other_half, own_half)):
-            db = None
-            for c in range(2):
-                dk, dv, dscores = block(keys[c], vals[c], keyt[c], s, c, bt0[s])
-                db = dscores if db is None else db + dscores
-                totals[c] = (dk, dv) if i == 0 else (totals[c][0] + dk, totals[c][1] + dv)
-            for tile in range(4):
-                top = db[0:72, 128 * tile : 128 * tile + 128]
-                bottom = db[72:144, 128 * tile : 128 * tile + 128]
-                owner = half_count * s + 2 * tile
-                sb0[owner] = jnp.where(lane, top, pltpu.roll(bottom, 64, 1)).astype(BF)
-                sb0[owner + 1] = jnp.where(lane, pltpu.roll(top, 64, 1), bottom).astype(BF)
-            send_bias(0, i)
-        for c in range(2):
-            for l in range(2):
-                gk[l, c] = totals[c][0][72 * l : 72 * l + 72]
-                gv[l, c] = totals[c][1][72 * l : 72 * l + 72]
-        finish(0)
-        grad_copies = send_grads((0,))
-
+        run(*[p0] * 6)
         arrived(1)
         arrived(2)
-        prepare(1)
-        for l in range(2):
-            for c in range(2):
-                part = normed[l, 72 * c : 72 * c + 72].astype(BF)
-                keys[2 + 2 * l + c, 0:72] = nn(part, wk[...]).astype(BF)
-                vals[2 + 2 * l + c, 0:72] = nn(part, wv[...]).astype(BF)
-                keyt[2 + 2 * l + c, :, 0:72] = (nt(wkt[...], part) * SCALE).astype(BF)
-        for i, s in enumerate((other_half, own_half)):
-            db = None
-            for c in range(2):
-                at = 2 + 2 * s + c
-                dk, dv, dscores = block(
-                    keys[at, 0:72], vals[at, 0:72], keyt[at, :, 0:72], s, c, bt1[s]
-                )
-                gk[s, c] = dk
-                gv[s, c] = dv
-                db = dscores if db is None else db + dscores
-            for tile in range(4):
-                part = db[:, 128 * tile : 128 * tile + 128]
-                top, bottom = part[0:40], part[32:72]
-                owner = half_count * s + 2 * tile
-                sb1[owner] = jnp.where(lane, top, pltpu.roll(bottom, 64, 1)).astype(BF)
-                sb1[owner + 1] = jnp.where(lane, pltpu.roll(top, 64, 1), bottom).astype(BF)
-            send_bias(1, i)
-        finish(1)
+        run(p1, b0, b1, p1, p1, b0, b2, p1, b1, b0, b3, p1, b1)
+        pack(0, 0)
+        run(p1, b2, b4, b2, b3, b5, b3)
+        pack(0, 1)
+        send_bias(0)
+        run(f0, b4, b6, f0)
+        grad_copies = send_grads((0,))
+        run(b4, b5, b7, b5, b6, b6, b7, b7, f1, f1)
         grad_copies += send_grads((1, 2))
+        pack(1, 0)
+        pack(1, 1)
+        send_bias(1)
 
         for copy in grad_copies:
             copy.wait()
         for a in range(2):
             keep_copy(a).wait()
 
-        def collect(slot, carry):
-            for a in range(2):
+        for a in range(2):
+            for slot in range(1, lon_count):
                 bias_copy(a, slot).wait()
-            return carry
-
-        lax.fori_loop(1, lon_count, collect, 0)
 
     return kernel
 
@@ -392,10 +423,10 @@
         parts = pl.pallas_call(
             make_kernel(lat_count, lon_count),
             out_shape=(
-                jax.ShapeDtypeStruct((OWNERS, 72, 128), BF),
-                jax.ShapeDtypeStruct((OWNERS, 40, 128), BF),
-                jax.ShapeDtypeStruct((4, 6, 3, 8, C), BF),
-                jax.ShapeDtypeStruct((4, 6, 8, C), BF),
+                pltpu.VMEM((OWNERS, 72, 128), BF),
+                pltpu.VMEM((OWNERS, 40, 128), BF),
+                pltpu.VMEM((4, 6, 3, 8, C), BF),
+                pltpu.VMEM((4, 6, 8, C), BF),
             ),
             in_specs=[any_spec] * 6,
             out_specs=(any_spec,) * 4,
@@ -408,25 +439,25 @@
                 pltpu.VMEM((72 * HEADS, HALF), BF),
                 pltpu.VMEM((72, HALF), BF),
                 pltpu.VMEM((C, HALF), BF),
-                pltpu.VMEM((2, 72, 192), BF),
-                pltpu.VMEM((2, 192, 72), BF),
+                pltpu.VMEM((144, 192), BF),
+                pltpu.VMEM((192, 144), BF),
                 pltpu.VMEM((1, C), F32),
                 pltpu.VMEM((C, 3 * C), BF),
                 pltpu.VMEM((C, C), BF),
             ]
-            + [pltpu.VMEM((C, C), BF)] * 5
+            + [pltpu.VMEM((C, C), BF)] * 3
             + [
-                pltpu.VMEM((2, 144, C), F32),
-                pltpu.VMEM((2, 144, C), F32),
-                pltpu.VMEM((2, 144, 1), F32),
-                pltpu.VMEM((2, 2, C, HALF), BF),
-                pltpu.VMEM((2, 2, C, HALF), BF),
+                pltpu.VMEM((2 * C, C), BF),
+                pltpu.VMEM((2, 2, 144, C), F32),
+                pltpu.VMEM((2, 2, 144, 1), F32),
+                pltpu.VMEM((2, 2, 2, C, HALF), BF),
+                pltpu.VMEM((2, 2, 2, C, HALF), BF),
                 pltpu.VMEM((6, 144, C), BF),
                 pltpu.VMEM((6, 144, C), BF),
                 pltpu.VMEM((6, C, 144), BF),
-                pltpu.VMEM((2, 2, 72, C), F32),
-                pltpu.VMEM((2, 2, 72, C), F32),
-                pltpu.VMEM((2, 2, 72, C), F32),
+                pltpu.VMEM((2, 2, 2, 72, C), F32),
+                pltpu.VMEM((2, 2, 2, 72, C), F32),
+                pltpu.VMEM((2, 2, 2, 72, C), F32),
                 pltpu.VMEM((4, 6, 4, 8, C), BF),
                 pltpu.VMEM((OWNERS, 72, 128), BF),
                 pltpu.VMEM((OWNERS, 40, 128), BF),
@@ -457,6 +488,7 @@
             ),
             in_specs=[vmem] * 4,
             out_specs=(vmem, vmem),
+            compiler_params=pltpu.CompilerParams(vmem_limit_bytes=8 * 1024 * 1024),
         )(*parts)
         return grad.reshape(4, 6, 24, C), bias_grad.reshape(2, 1, HEADS, 9, 144)
 

time: 42.9 us -> 40.7 us (0.949)
  the two profiles are of different devices: /device:TPU:2 before, /device:TPU:1 now
where the time goes in v3:
time: 40.7 us; the launch traced here: 40.5 us
  Pallas kernels  39.9 us (98%)
  between operations  0.64 us (2%)
    pallas_call x1, Pallas kernels, local(): pl.pallas_call(make_kernel(lat_count, lon_count), out_shape=(pltpu.VMEM((...  39 us
    pallas_call x1, Pallas kernels, local(): pl.pallas_call(make_final(lon_count), out_shape=(jax.ShapeDtypeStruct((4,...  0.88 us

profile of v3, /device:TPU:1, one launch (start us, length us, event | category | flops | bytes accessed | tf_op | source)
XLA Modules:
  0.0 40.5 jit_solution(9195797194870010078)
XLA Ops:
  0.6 39.0 %shard_map.77 = (bf16[16,72,128]{2,1,0:T(8,128)(2,1)S(1)}, bf16[16,40,128]{2,1,0:T(8,128)(2,1)S(1)}, bf16[4,6,3,8,192]{4,3,2,1,0:T(8,128)(2,1)S(1)}, bf16[4,6,8,192]{3,2,1,0:T(8,128)(2,1)S(1)}) custom-call(bf16[4,6,3,8,192]{4,3,2,1,0:T(8,128)(2,1)} %bitcast.7, bf16[4,6,3,8,192]{4,3,2,1,0:T(8,128)(2,1)} %bitcast.8, f32[1,192]{1,0:T(1,128)} %bitcast.9, ...), custom_call_target="tpu_custom_call" | custom-call | tf_op jit(solution)/shard_map/pallas_call | solution.py:423
  39.7 0.9 %shard_map.78 = (bf16[4,6,3,8,192]{4,3,2,1,0:T(8,128)(2,1)}, f32[2,6,9,1,144]{4,3,2,1,0:T(1,128)}) custom-call(bf16[16,72,128]{2,1,0:T(8,128)(2,1)S(1)} %get-tuple-element.8.rb0, bf16[16,40,128]{2,1,0:T(8,128)(2,1)S(1)} %get-tuple-element.9.rb1, bf16[4,6,3,8,192]{4,3,2,1,0:T(8,128)(2,1)S(1)} %get-tuple-element.10.gfull, ...), custom_call_target="tpu_custom_call" | custom-call | tf_op jit(solution)/shard_map/pallas_call | solution.py:483

commit v4 on v3

--- a/solution.py
+++ b/solution.py
@@ -48,13 +48,35 @@
     return 9 * (lane >> 6) + (lane & 63) - 9 * lane_head()
 
 
+def far_place(e):
+    row = (e * 57) >> 10
+    d = e - 56
+    edge_row = (d * 43) >> 8
+    return jnp.where(
+        e < 54,
+        24 * row + 6 + e - 18 * row,
+        jnp.where((d >= 0) & (d < 18), 24 * edge_row + d - 6 * edge_row, -1),
+    )
+
+
+def join(one, two):
+    tail = jnp.concatenate([one[:, 128:192], two[:, 128:192]], axis=1)
+    return [v.astype(BF).reshape(10, 8, 128) for v in (one[:, 0:128], two[:, 0:128], tail)]
+
+
+def split(ref, which):
+    return jnp.concatenate(
+        [ref[which].reshape(80, 128), ref[2].reshape(80, 128)[:, 64 * which : 64 * which + 64]], axis=1
+    )
+
+
 def make_kernel(lat_count, lon_count):
     def kernel(
-        tok, cot, gain_hbm, win_hbm, wout_hbm, bias_ref, rb0, rb1, gfull, edge,
-        x, bias_v, bt0, bt1, perm, permb, choose, mask, pcs, pct,
+        tok, cot, gain_hbm, win_hbm, wout_hbm, bias_ref, rb0, rb1, gr, near, edge,
+        x, far, fs, fr, ps, gs, bias_v, bt0, bt1, perm, permb, choose, mask, pcs, pct,
         gain_ref, win_ref, wout_ref, wq, wk, wv, wqkt,
         standard, inverse, qbd, ubd, keys, vals, keyt, gq, gk, gv, ext, sb0, sb1,
-        in_sem, own_sem, hs_sem, hr_sem, bs_sem, br_sem, gs_sem, gr_sem, keep_sem,
+        in_sem, own_sem, hs_sem, hr_sem, fs_sem, fr_sem, bs_sem, br_sem, gs_sem, gr_sem, keep_sem,
     ):
         lat = lax.axis_index("lat")
         lon = lax.axis_index("lon")
@@ -79,16 +101,23 @@
             pl.semaphore_signal(barrier, inc=1, device_id=there, device_id_type=MESH)
         lax.fori_loop(1, lon_count, greet, 0)
 
-        own_copies = [[], [], []]
+        own_copies, far_copies = [[], []], []
+        for g, (src, z, count) in enumerate(GROUPS):
+            for which, ref in enumerate((tok, cot)):
+                copy = pltpu.make_async_copy(
+                    ref.at[src : src + count, 0:3], far.at[which, z : z + count], own_sem.at[1, which, g]
+                )
+                copy.start()
+                far_copies.append(copy)
         for g, (src, z, count) in enumerate(GROUPS):
             for which, ref in enumerate((tok, cot)):
                 copy = pltpu.make_async_copy(
                     ref.at[src : src + count, 3:6],
-                    x.at[which, z : z + count, 0:3, 0:3],
-                    own_sem.at[which, g],
+                    x.at[which, z : z + count, :, 0:3],
+                    own_sem.at[0, which, g],
                 )
                 copy.start()
-                own_copies[g].append(copy)
+                own_copies[min(g, 1)].append(copy)
         in_copies = [
             pltpu.make_async_copy(source, target, in_sem.at[i])
             for i, (source, target) in enumerate(
@@ -104,28 +133,46 @@
         for copy in in_copies:
             copy.start()
 
+        ps[...] = one_hot(iota((80, 72), 1) == far_place(iota((80, 72), 0)))
+        for copy in far_copies:
+            copy.wait()
+        for z in range(4):
+            one, two = (nn(ps[...], far[which, z].reshape(72, C)) for which in range(2))
+            for i, v in enumerate(join(one, two)):
+                fs[z, i] = v
+
         pl.semaphore_wait(barrier, lon_count - 1 + 4)
 
-        halo_copies = [[], [], []]
-        for g, (src, z, count) in enumerate(GROUPS):
-            for which, ref in enumerate((tok, cot)):
-                for kind, (source, target, there) in enumerate(
-                    (
-                        (ref.at[src : src + count, 0:3, 0], x.at[which, z : z + count, 3:6, 3], (lat_prev, lon_prev)),
-                        (ref.at[src : src + count, 3:6, 0], x.at[which, z : z + count, 0:3, 3], (lat, lon_prev)),
-                        (ref.at[src : src + count, 0:3], x.at[which, z : z + count, 3:6, 0:3], (lat_prev, lon)),
+        halo_copies = [[], []]
+        for a in range(2):
+            span = pl.ds(2 * a, 2)
+            pieces = [
+                (fs.at[span, :, 7:10], fr.at[span, :, 7:10], (lat_prev, lon_prev), fs_sem.at[a, 0], fr_sem.at[a, 0]),
+                (fs.at[span, :, 0:7], fr.at[span, :, 0:7], (lat_prev, lon), fs_sem.at[a, 1], fr_sem.at[a, 1]),
+            ]
+            for g in ((1, 2) if a else (0,)):
+                src, z, count = GROUPS[g]
+                for which, ref in enumerate((tok, cot)):
+                    pieces.append(
+                        (
+                            ref.at[src : src + count, 3:6, 0],
+                            x.at[which, z : z + count, :, 3],
+                            (lat, lon_prev),
+                            hs_sem.at[which, g],
+                            hr_sem.at[which, g],
+                        )
                     )
-                ):
-                    copy = pltpu.make_async_remote_copy(
-                        src_ref=source,
-                        dst_ref=target,
-                        send_sem=hs_sem.at[which, kind, g],
-                        recv_sem=hr_sem.at[which, kind, g],
-                        device_id=there,
-                        device_id_type=MESH,
-                    )
-                    copy.start()
-                    halo_copies[g].append(copy)
+            for source, target, there, send_sem, recv_sem in pieces:
+                copy = pltpu.make_async_remote_copy(
+                    src_ref=source,
+                    dst_ref=target,
+                    send_sem=send_sem,
+                    recv_sem=recv_sem,
+                    device_id=there,
+                    device_id_type=MESH,
+                )
+                copy.start()
+                halo_copies[a].append(copy)
 
         heads, queries = lane_head(), lane_query()
         perm[...] = one_hot(iota((128 * HEADS, HALF), 0) == 128 * heads + queries)
@@ -136,10 +183,15 @@
             c = (token >= 72).astype(jnp.int32)
             inside = token - 72 * c
             row = (inside * 43) >> 9
-            return 32 * row + inside - 12 * row + 6 + 12 * c
-
-        pcs[...] = one_hot(iota((144, 192), 1) == grid_place(iota((144, 192), 0)))
-        pct[...] = one_hot(iota((192, 144), 0) == grid_place(iota((192, 144), 1)))
+            col = inside - 12 * row + 6 + 12 * c
+            return jnp.where(
+                row < 3,
+                32 * row + col,
+                96 + jnp.where(col < 24, 18 * row + col - 60, 6 * row + col + 14),
+            )
+
+        pcs[...] = one_hot(iota((144, 176), 1) == grid_place(iota((144, 176), 0)))
+        pct[...] = one_hot(iota((176, 144), 0) == grid_place(iota((176, 144), 1)))
         for copy in in_copies:
             copy.wait()
         wq[...] = win_ref[:, 0:192]
@@ -193,8 +245,18 @@
                     target[l, c] = jnp.concatenate([wide[at : at + 32]] * HEADS, axis=0) * mask[...]
 
         def prepare(a):
-            ts = [nn(pcs[...], x[0, 2 * a + l].reshape(192, C)) for l in range(2)]
-            cts = [nn(pcs[...], x[1, 2 * a + l].reshape(192, C)) for l in range(2)]
+            ts, cts = (
+                [
+                    nn(
+                        pcs[...],
+                        jnp.concatenate(
+                            [x[which, 2 * a + l].reshape(96, C), split(fr.at[2 * a + l], which)], axis=0
+                        ),
+                    )
+                    for l in range(2)
+                ]
+                for which in range(2)
+            )
             yield
             uts = [nt(wout_ref[...], pad_pair(cts[l])).astype(BF) for l in range(2)]
             plain = []
@@ -284,6 +346,7 @@
             dq, dk, dv = (ref[a].reshape(288, C).astype(BF) for ref in (gq, gk, gv))
             scaled = (nt(dq, wq[...]) + nt(dk, wk[...]) + nt(dv, wv[...])) * gain
             yield
+            away = []
             for l in range(2):
                 part = scaled[144 * l : 144 * l + 144]
                 unit = standard[a, l]
@@ -292,36 +355,37 @@
                     - jnp.sum(part, axis=-1, keepdims=True) * (1.0 / C)
                     - unit * (jnp.sum(part * unit, axis=-1, keepdims=True) * (1.0 / C))
                 )
-                ext[(2 * a + l + 1) % 4] = nn(pct[...], grad.astype(BF)).reshape(6, 4, 8, C).astype(BF)
-            yield
-
-        def send_grads(groups):
+                full = nn(pct[...], grad.astype(BF))
+                ext[(2 * a + l + 1) % 4] = full[0:96].reshape(3, 4, 8, C).astype(BF)
+                away.append(full[96:176])
+            for i, v in enumerate(join(*away)):
+                gs[a, i] = v
+            yield
+
+        def send_grads(a):
+            pieces = [
+                (gs.at[a, :, 0:7], gr.at[a, :, 0:7], (lat_next, lon), gs_sem.at[a, 0], gr_sem.at[a, 0]),
+                (gs.at[a, :, 7:10], gr.at[a, :, 7:10], (lat_next, lon_next), gs_sem.at[a, 1], gr_sem.at[a, 1]),
+            ]
             copies = []
-            for g in groups:
+            for g in ((1, 2) if a else (0,)):
                 level, _, count = GROUPS[g]
                 span = pl.ds(level, count)
-                for kind, (source, target, there) in enumerate(
-                    (
-                        (ext.at[span, 3:6, 3], edge.at[span, 0:3], (lat_next, lon_next)),
-                        (ext.at[span, 0:3, 3], edge.at[span, 3:6], (lat, lon_next)),
-                        (ext.at[span, 3:6, 0:3], gfull.at[span, 0:3], (lat_next, lon)),
-                    )
-                ):
-                    copies.append(
-                        pltpu.make_async_remote_copy(
-                            src_ref=source,
-                            dst_ref=target,
-                            send_sem=gs_sem.at[g, kind],
-                            recv_sem=gr_sem.at[g, kind],
-                            device_id=there,
-                            device_id_type=MESH,
-                        )
-                    )
-                copies.append(
-                    pltpu.make_async_copy(
-                        ext.at[span, 0:3, 0:3], gfull.at[span, 3:6], keep_sem.at[g]
-                    )
-                )
+                pieces.append(
+                    (ext.at[span, :, 3], edge.at[span], (lat, lon_next), gs_sem.at[2, g], gr_sem.at[2, g])
+                )
+                copies.append(pltpu.make_async_copy(ext.at[span, :, 0:3], near.at[span], keep_sem.at[g]))
+            copies = [
+                pltpu.make_async_remote_copy(
+                    src_ref=source,
+                    dst_ref=target,
+                    send_sem=send_sem,
+                    recv_sem=recv_sem,
+                    device_id=there,
+                    device_id_type=MESH,
+                )
+                for source, target, there, send_sem, recv_sem in pieces
+            ] + copies
             for copy in copies:
                 copy.start()
             return copies
@@ -364,16 +428,15 @@
         arrived(0)
         run(*[p0] * 6)
         arrived(1)
-        arrived(2)
         run(p1, b0, b1, p1, p1, b0, b2, p1, b1, b0, b3, p1, b1)
         pack(0, 0)
         run(p1, b2, b4, b2, b3, b5, b3)
         pack(0, 1)
         send_bias(0)
         run(f0, b4, b6, f0)
-        grad_copies = send_grads((0,))
+        grad_copies = send_grads(0)
         run(b4, b5, b7, b5, b6, b6, b7, b7, f1, f1)
-        grad_copies += send_grads((1, 2))
+        grad_copies += send_grads(1)
         pack(1, 0)
         pack(1, 1)
         send_bias(1)
@@ -391,10 +454,15 @@
 
 
 def make_final(lon_count):
-    def final(rb0, rb1, gfull, edge, out_ref, bout_ref):
+    def final(rb0, rb1, gr, near, edge, out_ref, bout_ref):
         lane = iota((1, 128), 1) < 64
-        out_ref[:, :, 1:3] = gfull[:, :, 1:3]
-        out_ref[:, :, 0] = gfull[:, :, 0] + edge[...]
+        out_ref[:, 3:6, 1:3] = near[:, :, 1:3]
+        out_ref[:, 3:6, 0] = near[:, :, 0] + edge[...]
+        back = one_hot(iota((72, 80), 0) == far_place(iota((72, 80), 1)))
+        for a in range(2):
+            for l in range(2):
+                rows = nn(back, split(gr.at[a], l))
+                out_ref[(2 * a + l + 1) % 4, 0:3] = rows.reshape(3, 3, 8, C).astype(BF)
         sum0, sum1 = rb0[0].astype(F32), rb1[0].astype(F32)
         for slot in range(1, lon_count):
             sum0 += rb0[slot].astype(F32)
@@ -425,13 +493,19 @@
             out_shape=(
                 pltpu.VMEM((OWNERS, 72, 128), BF),
                 pltpu.VMEM((OWNERS, 40, 128), BF),
-                pltpu.VMEM((4, 6, 3, 8, C), BF),
-                pltpu.VMEM((4, 6, 8, C), BF),
+                pltpu.VMEM((2, 3, 10, 8, 128), BF),
+                pltpu.VMEM((4, 3, 3, 8, C), BF),
+                pltpu.VMEM((4, 3, 8, C), BF),
             ),
             in_specs=[any_spec] * 6,
-            out_specs=(any_spec,) * 4,
+            out_specs=(any_spec,) * 5,
             scratch_shapes=[
-                pltpu.VMEM((2, 4, 6, 4, 8, C), BF),
+                pltpu.VMEM((2, 4, 3, 4, 8, C), BF),
+                pltpu.VMEM((2, 4, 3, 3, 8, C), BF),
+                pltpu.VMEM((4, 3, 10, 8, 128), BF),
+                pltpu.VMEM((4, 3, 10, 8, 128), BF),
+                pltpu.VMEM((80, 72), BF),
+                pltpu.VMEM((2, 3, 10, 8, 128), BF),
                 pltpu.VMEM((2, 864, 144), F32),
                 pltpu.VMEM((2, 144, HALF), F32),
                 pltpu.VMEM((2, 72, HALF), F32),
@@ -439,8 +513,8 @@
                 pltpu.VMEM((72 * HEADS, HALF), BF),
                 pltpu.VMEM((72, HALF), BF),
                 pltpu.VMEM((C, HALF), BF),
-                pltpu.VMEM((144, 192), BF),
-                pltpu.VMEM((192, 144), BF),
+                pltpu.VMEM((144, 176), BF),
+                pltpu.VMEM((176, 144), BF),
                 pltpu.VMEM((1, C), F32),
                 pltpu.VMEM((C, 3 * C), BF),
                 pltpu.VMEM((C, C), BF),
@@ -458,13 +532,15 @@
                 pltpu.VMEM((2, 2, 2, 72, C), F32),
                 pltpu.VMEM((2, 2, 2, 72, C), F32),
                 pltpu.VMEM((2, 2, 2, 72, C), F32),
-                pltpu.VMEM((4, 6, 4, 8, C), BF),
+                pltpu.VMEM((4, 3, 4, 8, C), BF),
                 pltpu.VMEM((OWNERS, 72, 128), BF),
                 pltpu.VMEM((OWNERS, 40, 128), BF),
                 dma((5,)),
+                dma((2, 2, 3)),
                 dma((2, 3)),
-                dma((2, 3, 3)),
-                dma((2, 3, 3)),
+                dma((2, 3)),
+                dma((2, 2)),
+                dma((2, 2)),
                 dma((2, OWNERS)),
                 dma((2, OWNERS)),
                 dma((3, 3)),
@@ -486,7 +562,7 @@
                 jax.ShapeDtypeStruct((4, 6, 3, 8, C), BF),
                 jax.ShapeDtypeStruct((2, HEADS, 9, 1, 144), F32),
             ),
-            in_specs=[vmem] * 4,
+            in_specs=[vmem] * 5,
             out_specs=(vmem, vmem),
             compiler_params=pltpu.CompilerParams(vmem_limit_bytes=8 * 1024 * 1024),
         )(*parts)

time: 40.7 us -> 40.7 us (level)
  no operation moved by 1% of the time
where the time goes in v4:
time: 40.7 us; the launch traced here: 40.5 us
  Pallas kernels  39.9 us (98%)
  between operations  0.64 us (2%)
    pallas_call x1, Pallas kernels, local(): pl.pallas_call(make_kernel(lat_count, lon_count), out_shape=(pltpu.VMEM((...  38.9 us
    pallas_call x1, Pallas kernels, local(): pl.pallas_call(make_final(lon_count), out_shape=(jax.ShapeDtypeStruct((4,...  0.99 us

profile of v4, /device:TPU:1, one launch (start us, length us, event | category | flops | bytes accessed | tf_op | source)
XLA Modules:
  0.0 40.5 jit_solution(16752393279689284782)
XLA Ops:
  0.6 38.9 %shard_map.77 = (bf16[16,72,128]{2,1,0:T(8,128)(2,1)S(1)}, bf16[16,40,128]{2,1,0:T(8,128)(2,1)S(1)}, bf16[2,3,10,8,128]{4,3,2,1,0:T(8,128)(2,1)S(1)}, bf16[4,3,3...) custom-call(bf16[4,6,3,8,192]{4,3,2,1,0:T(8,128)(2,1)} %bitcast.7, bf16[4,6,3,8,192]{4,3,2,1,0:T(8,128)(2,1)} %bitcast.8, ...), custom_call_target="tpu_custom_call" | custom-call | tf_op jit(solution)/shard_map/pallas_call | solution.py:491
  39.5 1.0 %shard_map.78 = (bf16[4,6,3,8,192]{4,3,2,1,0:T(8,128)(2,1)}, f32[2,6,9,1,144]{4,3,2,1,0:T(1,128)}) custom-call(bf16[16,72,128]{2,1,0:T(8,128)(2,1)S(1)} %get-tuple-element.9.rb0, bf16[16,40,128]{2,1,0:T(8,128)(2,1)S(1)} %get-tuple-element.10.rb1, bf16[2,3,10,8,128]{4,3,2,1,0:T(8,128)(2,1)S(1)} %get-tuple-element.11.gr, ...), custom_call_target="tpu_custom_call" | custom-call | tf_op jit(solution)/shard_map/pallas_call | solution.py:559

commit v5 on v4

--- a/solution.py
+++ b/solution.py
@@ -303,7 +303,10 @@
         sums = {}
         parts = {}
 
-        def block(a, s, c):
+        halves = (other_half, own_half)
+
+        def block(a, i, c):
+            s = halves[i]
             if a:
                 at = 2 + 2 * s + c
                 k, v, kt, biast = keys[at, 0:72], vals[at, 0:72], keyt[at, :, 0:72], bt1[s]
@@ -316,7 +319,7 @@
             probs = e * (1.0 / jnp.sum(e, axis=0, keepdims=True))
             weighted = probs * dprobs
             dscores = weighted - probs * jnp.sum(weighted, axis=0, keepdims=True)
-            sums[a, s] = dscores if c == 0 else sums[a, s] + dscores
+            sums[a, i] = dscores if c == 0 else sums[a, i] + dscores
             low = dscores.astype(BF)
             dv = nt(probs.astype(BF), ubd[a, s, c])
             wide = nn(kt, low)
@@ -324,7 +327,7 @@
             if a:
                 gk[a, s, c] = dk
                 gv[a, s, c] = dv
-            elif s == 0:
+            elif i == 0:
                 parts[c] = (dk, dv)
             else:
                 for target, total in ((gk, parts[c][0] + dk), (gv, parts[c][1] + dv)):
@@ -334,11 +337,11 @@
             gq[a, s, c] = nt(choose[...], wide.astype(BF) * mask[...])
             yield
 
-        def pack(a, s):
+        def pack(a, i):
             for tile in range(4):
-                part = sums[a, s][:, 128 * tile : 128 * tile + 128]
+                part = sums[a, i][:, 128 * tile : 128 * tile + 128]
                 target, top, bottom = (sb1, part[0:40], part[32:72]) if a else (sb0, part[0:72], part[72:144])
-                owner = 8 * s + 2 * tile
+                owner = 8 * halves[i] + 2 * tile
                 target[owner] = jnp.where(lane, top, pltpu.roll(bottom, 64, 1)).astype(BF)
                 target[owner + 1] = jnp.where(lane, pltpu.roll(top, 64, 1), bottom).astype(BF)
 
@@ -407,12 +410,11 @@
             source, target = ((sb0, rb0), (sb1, rb1))[a]
             return pltpu.make_async_copy(source.at[lon], target.at[0], keep_sem.at[3 + a])
 
-        def send_bias(a):
-            for slot in range(half_count, lon_count):
+        def send_bias(a, i):
+            for slot in range(1, half_count) if i else range(half_count, lon_count):
                 bias_copy(a, slot).start()
-            for slot in range(1, half_count):
-                bias_copy(a, slot).start()
-            keep_copy(a).start()
+            if i:
+                keep_copy(a).start()
 
         def arrived(g):
             for copy in own_copies[g] + halo_copies[g]:
@@ -423,23 +425,25 @@
                 next(piece)
 
         p0, p1, f0, f1 = prepare(0), prepare(1), finish(0), finish(1)
-        b0, b1, b2, b3 = (block(0, s, c) for s in range(2) for c in range(2))
-        b4, b5, b6, b7 = (block(1, s, c) for s in range(2) for c in range(2))
+        b0, b1, b2, b3 = (block(0, i, c) for i in range(2) for c in range(2))
+        b4, b5, b6, b7 = (block(1, i, c) for i in range(2) for c in range(2))
         arrived(0)
         run(*[p0] * 6)
         arrived(1)
         run(p1, b0, b1, p1, p1, b0, b2, p1, b1, b0, b3, p1, b1)
         pack(0, 0)
+        send_bias(0, 0)
         run(p1, b2, b4, b2, b3, b5, b3)
         pack(0, 1)
-        send_bias(0)
+        send_bias(0, 1)
         run(f0, b4, b6, f0)
         grad_copies = send_grads(0)
         run(b4, b5, b7, b5, b6, b6, b7, b7, f1, f1)
         grad_copies += send_grads(1)
         pack(1, 0)
         pack(1, 1)
-        send_bias(1)
+        send_bias(1, 0)
+        send_bias(1, 1)
 
         for copy in grad_copies:
             copy.wait()

time: 40.7 us -> 38.9 us (0.956)
  the two profiles are of different devices: /device:TPU:1 before, /device:TPU:2 now
where the time goes in v5:
time: 38.9 us; the launch traced here: 38.7 us
  Pallas kernels  38.1 us (98%)
  between operations  0.64 us (2%)
    pallas_call x1, Pallas kernels, local(): pl.pallas_call(make_kernel(lat_count, lon_count), out_shape=(pltpu.VMEM((...  37.1 us
    pallas_call x1, Pallas kernels, local(): pl.pallas_call(make_final(lon_count), out_shape=(jax.ShapeDtypeStruct((4,...  0.99 us

profile of v5, /device:TPU:2, one launch (start us, length us, event | category | flops | bytes accessed | tf_op | source)
XLA Modules:
  0.0 38.7 jit_solution(14265640914765471550)
XLA Ops:
  0.6 37.1 %shard_map.77 = (bf16[16,72,128]{2,1,0:T(8,128)(2,1)S(1)}, bf16[16,40,128]{2,1,0:T(8,128)(2,1)S(1)}, bf16[2,3,10,8,128]{4,3,2,1,0:T(8,128)(2,1)S(1)}, bf16[4,3,3...) custom-call(bf16[4,6,3,8,192]{4,3,2,1,0:T(8,128)(2,1)} %bitcast.7, bf16[4,6,3,8,192]{4,3,2,1,0:T(8,128)(2,1)} %bitcast.8, ...), custom_call_target="tpu_custom_call" | custom-call | tf_op jit(solution)/shard_map/pallas_call | solution.py:495
  37.8 1.0 %shard_map.78 = (bf16[4,6,3,8,192]{4,3,2,1,0:T(8,128)(2,1)}, f32[2,6,9,1,144]{4,3,2,1,0:T(1,128)}) custom-call(bf16[16,72,128]{2,1,0:T(8,128)(2,1)S(1)} %get-tuple-element.9.rb0, bf16[16,40,128]{2,1,0:T(8,128)(2,1)S(1)} %get-tuple-element.10.rb1, bf16[2,3,10,8,128]{4,3,2,1,0:T(8,128)(2,1)S(1)} %get-tuple-element.11.gr, ...), custom_call_target="tpu_custom_call" | custom-call | tf_op jit(solution)/shard_map/pallas_call | solution.py:563

commit v6 on v5

--- a/solution.py
+++ b/solution.py
@@ -429,16 +429,17 @@
         b4, b5, b6, b7 = (block(1, i, c) for i in range(2) for c in range(2))
         arrived(0)
         run(*[p0] * 6)
+        run(b0, b1)
         arrived(1)
-        run(p1, b0, b1, p1, p1, b0, b2, p1, b1, b0, b3, p1, b1)
+        run(p1, p1, b0, p1, b2, b1, p1, b3, b0, p1, b2, b1, p1)
         pack(0, 0)
         send_bias(0, 0)
-        run(p1, b2, b4, b2, b3, b5, b3)
+        run(b4, b3, b2, b5, b4, b3)
         pack(0, 1)
         send_bias(0, 1)
-        run(f0, b4, b6, f0)
+        run(b6, f0, b5, b7, b4, b6, f0)
         grad_copies = send_grads(0)
-        run(b4, b5, b7, b5, b6, b6, b7, b7, f1, f1)
+        run(b5, b7, b6, b7, f1, f1)
         grad_copies += send_grads(1)
         pack(1, 0)
         pack(1, 1)

time: 38.9 us -> 40.3 us (1.036)
  the two profiles are of different devices: /device:TPU:2 before, /device:TPU:1 now
where the time goes in v6:
time: 40.3 us; the launch traced here: 40.1 us
  Pallas kernels  39.5 us (98%)
  between operations  0.64 us (2%)
    pallas_call x1, Pallas kernels, local(): pl.pallas_call(make_kernel(lat_count, lon_count), out_shape=(pltpu.VMEM((...  38.5 us
    pallas_call x1, Pallas kernels, local(): pl.pallas_call(make_final(lon_count), out_shape=(jax.ShapeDtypeStruct((4,...  0.99 us

profile of v6, /device:TPU:1, one launch (start us, length us, event | category | flops | bytes accessed | tf_op | source)
XLA Modules:
  0.0 40.1 jit_solution(12304332629060666635)
XLA Ops:
  0.6 38.5 %shard_map.77 = (bf16[16,72,128]{2,1,0:T(8,128)(2,1)S(1)}, bf16[16,40,128]{2,1,0:T(8,128)(2,1)S(1)}, bf16[2,3,10,8,128]{4,3,2,1,0:T(8,128)(2,1)S(1)}, bf16[4,3,3...) custom-call(bf16[4,6,3,8,192]{4,3,2,1,0:T(8,128)(2,1)} %bitcast.7, bf16[4,6,3,8,192]{4,3,2,1,0:T(8,128)(2,1)} %bitcast.8, ...), custom_call_target="tpu_custom_call" | custom-call | tf_op jit(solution)/shard_map/pallas_call | solution.py:496
  39.1 1.0 %shard_map.78 = (bf16[4,6,3,8,192]{4,3,2,1,0:T(8,128)(2,1)}, f32[2,6,9,1,144]{4,3,2,1,0:T(1,128)}) custom-call(bf16[16,72,128]{2,1,0:T(8,128)(2,1)S(1)} %get-tuple-element.9.rb0, bf16[16,40,128]{2,1,0:T(8,128)(2,1)S(1)} %get-tuple-element.10.rb1, bf16[2,3,10,8,128]{4,3,2,1,0:T(8,128)(2,1)S(1)} %get-tuple-element.11.gr, ...), custom_call_target="tpu_custom_call" | custom-call | tf_op jit(solution)/shard_map/pallas_call | solution.py:564

commit v7 on v5

--- a/solution.py
+++ b/solution.py
@@ -429,16 +429,17 @@
         b4, b5, b6, b7 = (block(1, i, c) for i in range(2) for c in range(2))
         arrived(0)
         run(*[p0] * 6)
-        arrived(1)
-        run(p1, b0, b1, p1, p1, b0, b2, p1, b1, b0, b3, p1, b1)
+        run(b0, b1, b0, b2, b1, b3)
         pack(0, 0)
         send_bias(0, 0)
-        run(p1, b2, b4, b2, b3, b5, b3)
+        arrived(1)
+        run(b2, p1, b3, p1)
         pack(0, 1)
         send_bias(0, 1)
-        run(f0, b4, b6, f0)
+        run(b0, p1, b1, p1, b2, p1, b3, p1)
+        run(b4, b6, f0, b5, b4, b6, b7, b5, f0)
         grad_copies = send_grads(0)
-        run(b4, b5, b7, b5, b6, b6, b7, b7, f1, f1)
+        run(b4, b7, b5, b6, b7, f1, f1)
         grad_copies += send_grads(1)
         pack(1, 0)
         pack(1, 1)

time: 38.9 us -> 37.8 us (0.972)
  Pallas kernels: 38.1 us -> 36.9 us
    pallas_call x1, Pallas kernels: 37.1 us -> 36 us  [local(): pl.pallas_call(make_kernel(lat_count, lon_count), out_shape=(pltpu.VMEM((...]
where the time goes in v7:
time: 37.8 us; the launch traced here: 37.6 us
  Pallas kernels  36.9 us (98%)
  between operations  0.64 us (2%)
    pallas_call x1, Pallas kernels, local(): pl.pallas_call(make_kernel(lat_count, lon_count), out_shape=(pltpu.VMEM((...  36 us
    pallas_call x1, Pallas kernels, local(): pl.pallas_call(make_final(lon_count), out_shape=(jax.ShapeDtypeStruct((4,...  0.99 us

profile of v7, /device:TPU:2, one launch (start us, length us, event | category | flops | bytes accessed | tf_op | source)
XLA Modules:
  0.0 37.6 jit_solution(17120983738459688916)
XLA Ops:
  0.6 36.0 %shard_map.77 = (bf16[16,72,128]{2,1,0:T(8,128)(2,1)S(1)}, bf16[16,40,128]{2,1,0:T(8,128)(2,1)S(1)}, bf16[2,3,10,8,128]{4,3,2,1,0:T(8,128)(2,1)S(1)}, bf16[4,3,3...) custom-call(bf16[4,6,3,8,192]{4,3,2,1,0:T(8,128)(2,1)} %bitcast.7, bf16[4,6,3,8,192]{4,3,2,1,0:T(8,128)(2,1)} %bitcast.8, ...), custom_call_target="tpu_custom_call" | custom-call | tf_op jit(solution)/shard_map/pallas_call | solution.py:496
  36.6 1.0 %shard_map.78 = (bf16[4,6,3,8,192]{4,3,2,1,0:T(8,128)(2,1)}, f32[2,6,9,1,144]{4,3,2,1,0:T(1,128)}) custom-call(bf16[16,72,128]{2,1,0:T(8,128)(2,1)S(1)} %get-tuple-element.9.rb0, bf16[16,40,128]{2,1,0:T(8,128)(2,1)S(1)} %get-tuple-element.10.rb1, bf16[2,3,10,8,128]{4,3,2,1,0:T(8,128)(2,1)S(1)} %get-tuple-element.11.gr, ...), custom_call_target="tpu_custom_call" | custom-call | tf_op jit(solution)/shard_map/pallas_call | solution.py:564
